TPU v7x, 256 devices: a whole 4x4x8 slice. The times are simulated.
256 devices in a mesh: gx: 8 (over x, z_lo), gy: 32 (over y, z_hi, core).
Axes of the slice: x: 4, y: 4, z: 8 (z_hi: 4, z_lo: 2; z = z_hi * 2 + z_lo), core: 2. Of those that a mesh axis runs over, the one named last changes fastest.
Arguments:
- tokens: bfloat16 [512, 16384], P('gy', 'gx'), may hold values from -6 to 6
- gate_weight: bfloat16 [16384, 28672], P('gx', 'gy'), may hold values from -0.046875 to 0.046875
- up_weight: bfloat16 [16384, 28672], P('gx', 'gy'), may hold values from -0.046875 to 0.046875
- down_weight: bfloat16 [28672, 16384], P('gy', 'gx'), may hold values from -0.03125 to 0.03125
Outputs:
- mixed: bfloat16 [512, 16384], P('gy', 'gx')
All inputs are finite; a program needn't handle non-finite values.
Results may differ from a plain program's by a relative error of at most 0.025.
Values may be sent and summed in bfloat16 or wider, within the bound.
No kernel may reach another device: no remote copies, remote signals or barrier semaphores. Data moves between devices by JAX's collectives and lax.ppermute only.
A program may use at most 64 MiB of HBM per device.

v0:
```python
import jax
import jax.numpy as jnp
from jax import lax
from jax.sharding import PartitionSpec as P


def per_device(tokens, gate_weight, up_weight, down_weight):
    gathered = lax.all_gather(tokens, "gy", axis=0, tiled=True)
    width = gate_weight.shape[1]
    part = gathered
    gate_term = jnp.dot(part, gate_weight, preferred_element_type=jnp.float32)
    up_term = jnp.dot(part, up_weight, preferred_element_type=jnp.float32)
    summed = lax.psum_scatter(
        jnp.concatenate([gate_term, up_term], 1).astype(jnp.bfloat16),
        "gx",
        scatter_dimension=0,
        tiled=True,
    ).astype(jnp.float32)
    hidden_part = (jax.nn.silu(summed[:, :width]) * summed[:, width:]).astype(jnp.bfloat16)
    hidden = lax.all_gather(hidden_part, "gx", axis=0, tiled=True)
    part = hidden
    return lax.psum_scatter(
        jnp.dot(part, down_weight, preferred_element_type=jnp.float32).astype(jnp.bfloat16),
        "gy",
        scatter_dimension=0,
        tiled=True,
    )


def solution(mesh):
    in_specs = (P("gy", "gx"), P("gx", "gy"), P("gx", "gy"), P("gy", "gx"))
    out_specs = P("gy", "gx")
    return jax.shard_map(
        per_device, mesh=mesh, in_specs=in_specs, out_specs=out_specs, check_vma=False
    )
```

profile of v0, /device:TPU:2, one launch (start us, length us, event | category | flops | bytes accessed | tf_op | source)
XLA Modules:
  0.0 259.0 jit_solution(10418958684222920224)
XLA Ops:
  6.5 0.0 all-gather.2.cloned.1.call-start
  6.5 0.7 all-gather.2.cloned.1.call-update
  7.3 0.0 reduce-scatter.3.cloned.1.call-start
  7.3 60.4 %all-gather.2.cloned.1.call-done = bf16[512,2048]{1,0:T(8,128)(2,1)} async-done(((bf16[16,2048]{1,0:T(8,128)(2,1)}), bf16[512,2048]{1,0:T(8,128)(2,1)}) %all-gather.2.cloned.1.call-update) | async-done | bytes 2097168 | tf_op jit(solution)/shard_map/all_gather | solution.py:8
  67.7 0.0 copy-start
  67.7 0.0 copy-start.1
  67.7 5.1 %convolution_convert_fusion.1 = bf16[512,896]{1,0:T(8,128)(2,1)S(1)} fusion(bf16[512,2048]{1,0:T(8,128)(2,1)} %all-gather.2.cloned.1.call-done, bf16[2048,896]{1,0:T(8,128)(2,1)} %param.6), kind=kOutput, calls=%fused_computation.2 | convolution fusion | flops 1879506944 | bytes 6684672 | tf_op jit(solution)/shard_map/dot_general | solution.py:12
  72.8 0.0 copy-done
  72.8 0.0 copy-done.1
  72.8 2.4 convolution_convert_fusion.2
  75.2 1.4 pad_maximum_fusion
  76.6 0.0 reduce-scatter.3.cloned.1.call-update
  76.6 0.0 reduce-scatter.5.cloned.1.call-start
  76.7 45.5 %reduce-scatter.3.cloned.1.call-done = bf16[64,1792]{1,0:T(8,128)(2,1)} async-done(((bf16[512,1792]{1,0:T(8,128)(2,1)}), bf16[64,1792]{1,0:T(8,128)(2,1)}) %reduce-scatter.3.cloned.1.call-update) | async-done | bytes 229392 | tf_op jit(solution)/shard_map/reduce_scatter | solution.py:13
  122.2 1.0 convert_element_type.10
  123.1 0.1 fusion
  123.2 31.0 %all_gather.7 = bf16[512,896]{1,0:T(8,128)(2,1)S(1)} all-gather(bf16[64,896]{1,0:T(8,128)(2,1)S(1)} %fusion), channel_id=1, replica_groups=mesh['gx'=8,'gy'=32] {'gx'}, dimensions={0}, use_global_device_ids=true | all-gather | bytes 1032192 | tf_op jit(solution)/shard_map/all_gather | solution.py:20
  154.2 5.8 %convolution_convert_fusion = bf16[512,2048]{1,0:T(8,128)(2,1)} fusion(bf16[512,896]{1,0:T(8,128)(2,1)S(1)} %all_gather.7, bf16[896,2048]{1,0:T(8,128)(2,1)} %param.7), kind=kOutput, calls=%fused_computation | convolution fusion | flops 1880096768 | bytes 6684672 | tf_op jit(solution)/shard_map/dot_general | solution.py:23
  160.0 0.0 reduce-scatter.5.cloned.1.call-update
  160.0 92.5 %reduce-scatter.5.cloned.1.call-done = bf16[16,2048]{1,0:T(8,128)(2,1)} async-done(((bf16[512,2048]{1,0:T(8,128)(2,1)}), bf16[16,2048]{1,0:T(8,128)(2,1)}) %reduce-scatter.5.cloned.1.call-update) | async-done | bytes 65552 | tf_op jit(solution)/shard_map/reduce_scatter | solution.py:22
Async XLA Ops:
  6.5 61.1 %all-gather.2.cloned.1.call-start = ((), (), s32[]{:S(2)}) async-start(), calls=%async_computation.2 | async-start | bytes 2162688 | tf_op jit(solution)/shard_map/all_gather | solution.py:8
  7.3 114.9 %reduce-scatter.3.cloned.1.call-start = ((), (), s32[]{:S(2)}) async-start(), calls=%async_computation.3 | async-start | bytes 2064384 | tf_op jit(solution)/shard_map/reduce_scatter | solution.py:13
  67.7 5.2 %copy-start = (bf16[2048,896]{1,0:T(8,128)(2,1)S(1)}, bf16[2048,896]{1,0:T(8,128)(2,1)}, u32[]{:S(2)}) copy-start(bf16[2048,896]{1,0:T(8,128)(2,1)} %param.5) | copy-start | bytes 11010052
  67.7 5.2 %copy-start.1 = (bf16[512,2048]{1,0:T(8,128)(2,1)S(1)}, bf16[512,2048]{1,0:T(8,128)(2,1)}, u32[]{:S(2)}) copy-start(bf16[512,2048]{1,0:T(8,128)(2,1)} %all-gather.2.cloned.1.call-done) | copy-start | bytes 6291460
  76.6 175.9 %reduce-scatter.5.cloned.1.call-start = ((), (), s32[]{:S(2)}) async-start(), calls=%async_computation.4 | async-start | bytes 2162688 | tf_op jit(solution)/shard_map/reduce_scatter | solution.py:22
Sparse Core Ops, SparseCore 0:
  9.9 57.7 all-gather.1
  76.7 45.3 reduce-scatter.2
  160.1 92.3 reduce-scatter.4
where the time goes:
time: 259 us
  waiting for transfers between devices  199 us (77%)
  blocking collectives  31 us (12%)
  matrix products  13.2 us (5%)
  between operations  13.2 us (5%)
    reduce_scatter x1, waiting for transfers between devices, per_device(): lax.psum_scatter(jnp.dot(part, down_weight, preferred_element_type=jnp.fl...  92.5 us
    all_gather x1, waiting for transfers between devices, per_device(): gathered = lax.all_gather(tokens, 'gy', axis=0, tiled=True)  60.4 us
    reduce_scatter x1, waiting for transfers between devices, per_device(): lax.psum_scatter(jnp.concatenate([gate_term, up_term], 1).astype(jnp.bflo...  45.5 us
    all_gather x1, blocking collectives, per_device(): hidden = lax.all_gather(hidden_part, 'gx', axis=0, tiled=True)  31 us
    dot_general x1, matrix products, per_device(): jnp.dot(part, down_weight, preferred_element_type=jnp.float32)  5.75 us
  transfers between devices with their start and end apart: 3, of which 3 were waited for; matrix products, arithmetic and copies ran while one was open for 0% of the time, Pallas kernels for 0%

commit v1 on v0

v1 whole, which is shorter than its diff:
```python
import jax
import jax.numpy as jnp
from jax import lax
from jax.sharding import PartitionSpec as P

CORES, Z_PARTS, Y_PARTS = 2, 4, 4


def swap(value, step):
    size = CORES * Z_PARTS * Y_PARTS
    return lax.ppermute(value, "gy", [(a, a ^ step) for a in range(size)])


def gather_steps(value, unit, parts):
    return jnp.concatenate([value] + [swap(value, unit * i) for i in range(1, parts)], 0)


def reduce_steps(value, unit, parts):
    rows = value.shape[0] // parts
    pieces = [value[i * rows:(i + 1) * rows] for i in range(parts)]
    total = pieces[0].astype(jnp.float32)
    for i in range(1, parts):
        total = total + swap(pieces[i], unit * i).astype(jnp.float32)
    return total.astype(jnp.bfloat16)


def per_device(tokens, gate_weight, up_weight, down_weight):
    width = gate_weight.shape[1]
    groups = lax.axis_size("gx")
    both = jnp.concatenate([gate_weight, up_weight], 1)
    part = gather_steps(tokens, CORES, Z_PARTS)
    part = gather_steps(part, CORES * Z_PARTS, Y_PARTS)
    part = gather_steps(part, 1, CORES)
    term = jnp.dot(part, both, preferred_element_type=jnp.float32).astype(jnp.bfloat16)
    rows = term.shape[0] // groups
    terms = lax.all_to_all(term.reshape(groups, rows, 2 * width), "gx", 0, 0)
    summed = terms.astype(jnp.float32).sum(0)
    hidden_part = (jax.nn.silu(summed[:, :width]) * summed[:, width:]).astype(jnp.bfloat16)
    hidden = lax.all_to_all(
        jnp.broadcast_to(hidden_part[None], (groups, rows, width)), "gx", 0, 0
    ).reshape(groups * rows, width)
    half = hidden.shape[0] // 2
    theirs = jnp.dot(hidden[half:], down_weight, preferred_element_type=jnp.float32).astype(jnp.bfloat16)
    came = swap(theirs, 1)
    mine = jnp.dot(hidden[:half], down_weight, preferred_element_type=jnp.float32)
    out = (mine + came.astype(jnp.float32)).astype(jnp.bfloat16)
    out = reduce_steps(out, CORES * Z_PARTS, Y_PARTS)
    return reduce_steps(out, CORES, Z_PARTS)


def solution(mesh):
    in_specs = (P("gy", "gx"), P("gx", "gy"), P("gx", "gy"), P("gy", "gx"))
    out_specs = P("gy", "gx")
    return jax.shard_map(
        per_device, mesh=mesh, in_specs=in_specs, out_specs=out_specs, check_vma=False
    )
```

time: 259 us -> 124 us (0.48)
  waiting for transfers between devices: 199 us -> 41.6 us
  starting transfers between devices: 0.08 us -> 25.2 us
  blocking collectives: 31 us -> 44.5 us
  between operations: 13.2 us -> 0.18 us
  matrix products: 13.2 us -> 8.54 us
    reduce_scatter x2 -> x0, waiting for transfers between devices: 138 us -> none  [the longest x1 92.5 us: per_device(): lax.psum_scatter(jnp.dot(part, down_weight, preferred_element_type=jnp.fl...]
    all_gather x1 -> x0, waiting for transfers between devices: 60.4 us -> none  [per_device(): gathered = lax.all_gather(tokens, 'gy', axis=0, tiled=True)]
    all_to_all x0 -> x2, blocking collectives: none -> 44.5 us  [the longest x1 27.7 us: per_device(): terms = lax.all_to_all(term.reshape(groups, rows, 2 * width), 'gx', 0, 0)]
    ppermute x0 -> x14, waiting for transfers between devices: none -> 41.6 us  [swap(): return lax.ppermute(value, 'gy', [(a, a ^ step) for a in range(size)])]
    all_gather x1 -> x0, blocking collectives: 31 us -> none  [per_device(): hidden = lax.all_gather(hidden_part, 'gx', axis=0, tiled=True)]
    ppermute x0 -> x14, starting transfers between devices: none -> 25.2 us  [swap(): return lax.ppermute(value, 'gy', [(a, a ^ step) for a in range(size)])]
    dot_general x3, matrix products: 13.2 us -> 8.54 us  [the longest x1 6.03 us: per_device(): jnp.dot(part, both, preferred_element_type=jnp.float32).astype(jnp.bfloat16)]
  transfers between devices with their start and end apart: 3 -> 14, of which waited for: 3 -> 11; matrix products, arithmetic and copies ran while one was open for 0% -> 1% of each run, Pallas kernels for 0% -> 0%
where the time goes in v1:
time: 124 us; the launch traced here: 123 us
  blocking collectives  44.5 us (36%)
  waiting for transfers between devices  41.6 us (34%)
  starting transfers between devices  25.2 us (20%)
  matrix products  8.54 us (7%)
  local copies, waits for them, and re-layouts  1.44 us (1%)
    ppermute x14, waiting for transfers between devices, swap(): return lax.ppermute(value, 'gy', [(a, a ^ step) for a in range(size)])  41.6 us
    all_to_all x1, blocking collectives, per_device(): terms = lax.all_to_all(term.reshape(groups, rows, 2 * width), 'gx', 0, 0)  27.7 us
    ppermute x14, starting transfers between devices, swap(): return lax.ppermute(value, 'gy', [(a, a ^ step) for a in range(size)])  25.2 us
    all_to_all x1, blocking collectives, per_device(): lax.all_to_all(jnp.broadcast_to(hidden_part[None], (groups, rows, width))...  16.8 us
    dot_general x1, matrix products, per_device(): jnp.dot(part, both, preferred_element_type=jnp.float32).astype(jnp.bfloat16)  6.03 us
  transfers between devices with their start and end apart: 14, of which 11 were waited for; matrix products, arithmetic and copies ran while one was open for 1% of the time, Pallas kernels for 0%

profile of v1, /device:TPU:2, one launch (start us, length us, event | category | flops | bytes accessed | tf_op | source)
XLA Modules:
  0.0 122.5 jit_solution(4868490755471670568)
XLA Ops:
  0.0 3.3 %collective-permute-start = (bf16[16,2048]{1,0:T(8,128)(2,1)}, bf16[16,2048]{1,0:T(8,128)(2,1)S(1)}, u32[]{:S(2)}, u32[]{:S(2)}) collective-permute-start(bf16[16,2048]{1,0:T(8,128)(2,1)} %param.4), channel_id=1, source_target_pairs={{0,2},{1,3},{2,0},{3,1},{4,6},{5,7},{6,4},{7,5},{8,10},{9,11},{10,... | collective-permute-start | bytes 196616 | tf_op jit(solution)/shard_map/ppermute | solution.py:11
  3.3 5.4 %collective-permute-start.1 = (bf16[16,2048]{1,0:T(8,128)(2,1)}, bf16[16,2048]{1,0:T(8,128)(2,1)S(1)}, u32[]{:S(2)}, u32[]{:S(2)}) collective-permute-start(bf16[16,2048]{1,0:T(8,128)(2,1)} %param.4), channel_id=1, source_target_pairs={{0,4},{1,5},{2,6},{3,7},{4,0},{5,1},{6,2},{7,3},{8,12},{9,13},{10,... | collective-permute-start | bytes 196616 | tf_op jit(solution)/shard_map/ppermute | solution.py:11
  8.7 0.0 collective-permute-start.2
  8.7 0.9 constant_dynamic-update-slice_fusion.10
  9.6 0.0 collective-permute-done
  9.6 2.6 %collective-permute-done.1 = bf16[16,2048]{1,0:T(8,128)(2,1)S(1)} collective-permute-done((bf16[16,2048]{1,0:T(8,128)(2,1)}, bf16[16,2048]{1,0:T(8,128)(2,1)S(1)}, u32[]{:S(2)}, u32[]{:S(2)}) %collective-permute-start.1) | collective-permute-done | bytes 65568 | tf_op jit(solution)/shard_map/ppermute | solution.py:11
  12.2 3.0 %collective-permute-done.2 = bf16[16,2048]{1,0:T(8,128)(2,1)S(1)} collective-permute-done((bf16[16,2048]{1,0:T(8,128)(2,1)}, bf16[16,2048]{1,0:T(8,128)(2,1)S(1)}, u32[]{:S(2)}, u32[]{:S(2)}) %collective-permute-start.2) | collective-permute-done | bytes 65568 | tf_op jit(solution)/shard_map/ppermute | solution.py:11
  15.3 1.7 %collective-permute-start.3 = (bf16[64,2048]{1,0:T(8,128)(2,1)S(1)}, bf16[64,2048]{1,0:T(8,128)(2,1)S(1)}, u32[]{:S(2)}, u32[]{:S(2)}) collective-permute-start(bf16[64,2048]{1,0:T(8,128)(2,1)S(1)} %get-tuple-element.21), channel_id=1, source_target_pairs={{0,8},{1,9},{2,10},{3,11},{4,12},{5,13},{6,14},{7,15},{8,0},{9,1},... | collective-permute-start | bytes 786440 | tf_op jit(solution)/shard_map/ppermute | solution.py:11
  16.9 2.9 %collective-permute-start.4 = (bf16[64,2048]{1,0:T(8,128)(2,1)S(1)}, bf16[64,2048]{1,0:T(8,128)(2,1)S(1)}, u32[]{:S(2)}, u32[]{:S(2)}) collective-permute-start(bf16[64,2048]{1,0:T(8,128)(2,1)S(1)} %get-tuple-element.21), channel_id=1, source_target_pairs={{0,16},{1,17},{2,18},{3,19},{4,20},{5,21},{6,22},{7,23},{8,24},{9,... | collective-permute-start | bytes 786440 | tf_op jit(solution)/shard_map/ppermute | solution.py:11
  19.8 0.2 collective-permute-start.5
  20.1 4.5 %collective-permute-done.3 = bf16[64,2048]{1,0:T(8,128)(2,1)S(1)} collective-permute-done((bf16[64,2048]{1,0:T(8,128)(2,1)S(1)}, bf16[64,2048]{1,0:T(8,128)(2,1)S(1)}, u32[]{:S(2)}, u32[]{:S(2)}) %collective-permute-start.3) | collective-permute-done | bytes 262176 | tf_op jit(solution)/shard_map/ppermute | solution.py:11
  24.6 0.0 copy-start
  24.7 5.6 %collective-permute-done.4 = bf16[64,2048]{1,0:T(8,128)(2,1)S(1)} collective-permute-done((bf16[64,2048]{1,0:T(8,128)(2,1)S(1)}, bf16[64,2048]{1,0:T(8,128)(2,1)S(1)}, u32[]{:S(2)}, u32[]{:S(2)}) %collective-permute-start.4) | collective-permute-done | bytes 262176 | tf_op jit(solution)/shard_map/ppermute | solution.py:11
  30.3 2.5 %collective-permute-done.5 = bf16[64,2048]{1,0:T(8,128)(2,1)S(1)} collective-permute-done((bf16[64,2048]{1,0:T(8,128)(2,1)S(1)}, bf16[64,2048]{1,0:T(8,128)(2,1)S(1)}, u32[]{:S(2)}, u32[]{:S(2)}) %collective-permute-start.5) | collective-permute-done | bytes 262176 | tf_op jit(solution)/shard_map/ppermute | solution.py:11
  32.9 0.1 collective-permute-start.6
  33.0 2.6 %collective-permute-done.6 = bf16[256,2048]{1,0:T(8,128)(2,1)S(1)} collective-permute-done((bf16[256,2048]{1,0:T(8,128)(2,1)S(1)}, bf16[256,2048]{1,0:T(8,128)(2,1)S(1)}, u32[]{:S(2)}, u32[]{:S(2)}) %collective-permute-start.6) | collective-permute-done | bytes 1048608 | tf_op jit(solution)/shard_map/ppermute | solution.py:11
  35.6 0.1 constant_dynamic-update-slice_fusion.11
  35.7 0.0 copy-done
  35.7 6.0 %fusion.4 = bf16[512,1792]{1,0:T(8,128)(2,1)S(1)} fusion(bf16[512,2048]{1,0:T(8,128)(2,1)S(1)} %constant_dynamic-update-slice_fusion.11, bf16[2048,896]{1,0:T(8,128)(2,1)S(1)} %copy-done, bf16[2048,896]{1,0:T(8,128)(2,1)} %param.5), kind=kOutput, calls=%fused_computation.5 | convolution fusion | flops 3773693952 | bytes 11272192 | tf_op jit(solution)/shard_map/dot_general | solution.py:34
  41.7 27.7 %all_to_all.10 = bf16[8,64,1792]{2,1,0:T(8,128)(2,1)S(1)} all-to-all(bf16[8,64,1792]{2,1,0:T(8,128)(2,1)S(1)} %bitcast.8), channel_id=1, replica_groups=mesh['gx'=8,'gy'=32] {'gx'}, dimensions={0} | all-to-all | bytes 3670016 | tf_op jit(solution)/shard_map/all_to_all | solution.py:36
  69.4 0.2 convert_reduce_fusion
  69.7 0.1 fusion.7
  69.7 0.0 copy-start.1
  69.7 0.1 broadcast_in_dim.2
  69.9 16.8 %all_to_all.11 = bf16[8,64,896]{2,1,0:T(8,128)(2,1)S(1)} all-to-all(bf16[8,64,896]{2,1,0:T(8,128)(2,1)S(1)} %broadcast_in_dim.2), channel_id=1, replica_groups=mesh['gx'=8,'gy'=32] {'gx'}, dimensions={0} | all-to-all | bytes 1835008 | tf_op jit(solution)/shard_map/all_to_all | solution.py:39
  86.7 0.1 fusion.10
  86.8 0.0 copy-done.1
  86.8 1.3 %convolution_convert_fusion = bf16[256,2048]{1,0:T(8,128)(2,1)S(1)} fusion(bf16[256,896]{1,0:T(8,128)(2,1)S(1)} %bitcast.10, bf16[896,2048]{1,0:T(8,128)(2,1)S(1)} %copy-done.1), kind=kOutput, calls=%fused_computation.6 | convolution fusion | flops 940048384 | bytes 5177344 | tf_op jit(solution)/shard_map/dot_general | solution.py:43
  88.1 0.1 collective-permute-start.7
  88.2 2.6 %collective-permute-done.7 = bf16[256,2048]{1,0:T(8,128)(2,1)S(1)} collective-permute-done((bf16[256,2048]{1,0:T(8,128)(2,1)S(1)}, bf16[256,2048]{1,0:T(8,128)(2,1)S(1)}, u32[]{:S(2)}, u32[]{:S(2)}) %collective-permute-start.7) | collective-permute-done | bytes 1048608 | tf_op jit(solution)/shard_map/ppermute | solution.py:11
  90.8 1.3 %add_convert_fusion = bf16[256,2048]{1,0:T(8,128)(2,1)S(1)} fusion(bf16[256,2048]{1,0:T(8,128)(2,1)S(1)} %collective-permute-done.7, bf16[256,896]{1,0:T(8,128)(2,1)S(1)} %bitcast.9, bf16[896,2048]{1,0:T(8,128)(2,1)S(1)} %copy-done.1), kind=kOutput, calls=%fused_computation.7 | convolution fusion | flops 941096960 | bytes 6225920 | tf_op jit(solution)/shard_map/dot_general | solution.py:45
  92.1 0.1 fusion.9
  92.1 0.4 collective-permute-start.10
  92.5 0.0 collective-permute-start.8
  92.5 4.4 %collective-permute-start.9 = (bf16[64,2048]{1,0:T(8,128)(2,1)S(1)}, bf16[64,2048]{1,0:T(8,128)(2,1)S(1)}, u32[]{:S(2)}, u32[]{:S(2)}) collective-permute-start(bf16[64,2048]{1,0:T(8,128)(2,1)S(1)} %get-tuple-element.7), channel_id=1, source_target_pairs={{0,16},{1,17},{2,18},{3,19},{4,20},{5,21},{6,22},{7,23},{8,24},{9,... | collective-permute-start | bytes 786440 | tf_op jit(solution)/shard_map/ppermute | solution.py:11
  96.9 4.9 %collective-permute-done.10 = bf16[64,2048]{1,0:T(8,128)(2,1)S(1)} collective-permute-done((bf16[64,2048]{1,0:T(8,128)(2,1)S(1)}, bf16[64,2048]{1,0:T(8,128)(2,1)S(1)}, u32[]{:S(2)}, u32[]{:S(2)}) %collective-permute-start.10) | collective-permute-done | bytes 262176 | tf_op jit(solution)/shard_map/ppermute | solution.py:11
  101.8 0.0 collective-permute-done.8
  101.8 6.8 %collective-permute-done.9 = bf16[64,2048]{1,0:T(8,128)(2,1)S(1)} collective-permute-done((bf16[64,2048]{1,0:T(8,128)(2,1)S(1)}, bf16[64,2048]{1,0:T(8,128)(2,1)S(1)}, u32[]{:S(2)}, u32[]{:S(2)}) %collective-permute-start.9) | collective-permute-done | bytes 262176 | tf_op jit(solution)/shard_map/ppermute | solution.py:11
  108.6 0.1 add_convert_fusion.1
  108.7 2.1 %collective-permute-start.11 = (bf16[16,2048]{1,0:T(8,128)(2,1)S(1)}, bf16[16,2048]{1,0:T(8,128)(2,1)S(1)}, u32[]{:S(2)}, u32[]{:S(2)}) collective-permute-start(bf16[16,2048]{1,0:T(8,128)(2,1)S(1)} %get-tuple-element.10), channel_id=1, source_target_pairs={{0,2},{1,3},{2,0},{3,1},{4,6},{5,7},{6,4},{7,5},{8,10},{9,11},{10,... | collective-permute-start | bytes 196616 | tf_op jit(solution)/shard_map/ppermute | solution.py:11
  110.8 4.6 %collective-permute-start.12 = (bf16[16,2048]{1,0:T(8,128)(2,1)S(1)}, bf16[16,2048]{1,0:T(8,128)(2,1)S(1)}, u32[]{:S(2)}, u32[]{:S(2)}) collective-permute-start(bf16[16,2048]{1,0:T(8,128)(2,1)S(1)} %get-tuple-element.12), channel_id=1, source_target_pairs={{0,4},{1,5},{2,6},{3,7},{4,0},{5,1},{6,2},{7,3},{8,12},{9,13},{10,... | collective-permute-start | bytes 196616 | tf_op jit(solution)/shard_map/ppermute | solution.py:11
  115.4 0.1 collective-permute-start.13
  115.5 0.0 collective-permute-done.11
  115.5 3.7 %collective-permute-done.12 = bf16[16,2048]{1,0:T(8,128)(2,1)S(1)} collective-permute-done((bf16[16,2048]{1,0:T(8,128)(2,1)S(1)}, bf16[16,2048]{1,0:T(8,128)(2,1)S(1)}, u32[]{:S(2)}, u32[]{:S(2)}) %collective-permute-start.12) | collective-permute-done | bytes 65568 | tf_op jit(solution)/shard_map/ppermute | solution.py:11
  119.1 2.7 %collective-permute-done.13 = bf16[16,2048]{1,0:T(8,128)(2,1)S(1)} collective-permute-done((bf16[16,2048]{1,0:T(8,128)(2,1)S(1)}, bf16[16,2048]{1,0:T(8,128)(2,1)S(1)}, u32[]{:S(2)}, u32[]{:S(2)}) %collective-permute-start.13) | collective-permute-done | bytes 65568 | tf_op jit(solution)/shard_map/ppermute | solution.py:11
  121.9 0.7 add_convert_fusion.2
  (7 shorter events, 0.2 us)
Async XLA Ops:
  0.0 9.6 %collective-permute-start = (bf16[16,2048]{1,0:T(8,128)(2,1)}, bf16[16,2048]{1,0:T(8,128)(2,1)S(1)}, u32[]{:S(2)}, u32[]{:S(2)}) collective-permute-start(bf16[16,2048]{1,0:T(8,128)(2,1)} %param.4), channel_id=1, source_target_pairs={{0,2},{1,3},{2,0},{3,1},{4,6},{5,7},{6,4},{7,5},{8,10},{9,11},{10,... | collective-permute-start | bytes 196616 | tf_op jit(solution)/shard_map/ppermute | solution.py:11
  3.3 8.9 %collective-permute-start.1 = (bf16[16,2048]{1,0:T(8,128)(2,1)}, bf16[16,2048]{1,0:T(8,128)(2,1)S(1)}, u32[]{:S(2)}, u32[]{:S(2)}) collective-permute-start(bf16[16,2048]{1,0:T(8,128)(2,1)} %param.4), channel_id=1, source_target_pairs={{0,4},{1,5},{2,6},{3,7},{4,0},{5,1},{6,2},{7,3},{8,12},{9,13},{10,... | collective-permute-start | bytes 196616 | tf_op jit(solution)/shard_map/ppermute | solution.py:11
  8.7 6.6 %collective-permute-start.2 = (bf16[16,2048]{1,0:T(8,128)(2,1)}, bf16[16,2048]{1,0:T(8,128)(2,1)S(1)}, u32[]{:S(2)}, u32[]{:S(2)}) collective-permute-start(bf16[16,2048]{1,0:T(8,128)(2,1)} %param.4), channel_id=1, source_target_pairs={{0,6},{1,7},{2,4},{3,5},{4,2},{5,3},{6,0},{7,1},{8,14},{9,15},{10,... | collective-permute-start | bytes 196616 | tf_op jit(solution)/shard_map/ppermute | solution.py:11
  15.3 9.3 %collective-permute-start.3 = (bf16[64,2048]{1,0:T(8,128)(2,1)S(1)}, bf16[64,2048]{1,0:T(8,128)(2,1)S(1)}, u32[]{:S(2)}, u32[]{:S(2)}) collective-permute-start(bf16[64,2048]{1,0:T(8,128)(2,1)S(1)} %get-tuple-element.21), channel_id=1, source_target_pairs={{0,8},{1,9},{2,10},{3,11},{4,12},{5,13},{6,14},{7,15},{8,0},{9,1},... | collective-permute-start | bytes 786440 | tf_op jit(solution)/shard_map/ppermute | solution.py:11
  16.9 13.3 %collective-permute-start.4 = (bf16[64,2048]{1,0:T(8,128)(2,1)S(1)}, bf16[64,2048]{1,0:T(8,128)(2,1)S(1)}, u32[]{:S(2)}, u32[]{:S(2)}) collective-permute-start(bf16[64,2048]{1,0:T(8,128)(2,1)S(1)} %get-tuple-element.21), channel_id=1, source_target_pairs={{0,16},{1,17},{2,18},{3,19},{4,20},{5,21},{6,22},{7,23},{8,24},{9,... | collective-permute-start | bytes 786440 | tf_op jit(solution)/shard_map/ppermute | solution.py:11
  19.8 13.0 %collective-permute-start.5 = (bf16[64,2048]{1,0:T(8,128)(2,1)S(1)}, bf16[64,2048]{1,0:T(8,128)(2,1)S(1)}, u32[]{:S(2)}, u32[]{:S(2)}) collective-permute-start(bf16[64,2048]{1,0:T(8,128)(2,1)S(1)} %get-tuple-element.21), channel_id=1, source_target_pairs={{0,24},{1,25},{2,26},{3,27},{4,28},{5,29},{6,30},{7,31},{8,16},{9,... | collective-permute-start | bytes 786440 | tf_op jit(solution)/shard_map/ppermute | solution.py:11
  24.6 11.1 %copy-start = (bf16[2048,896]{1,0:T(8,128)(2,1)S(1)}, bf16[2048,896]{1,0:T(8,128)(2,1)}, u32[]{:S(2)}) copy-start(bf16[2048,896]{1,0:T(8,128)(2,1)} %param.6) | copy-start | bytes 11010052
  32.9 2.7 %collective-permute-start.6 = (bf16[256,2048]{1,0:T(8,128)(2,1)S(1)}, bf16[256,2048]{1,0:T(8,128)(2,1)S(1)}, u32[]{:S(2)}, u32[]{:S(2)}) collective-permute-start(bf16[256,2048]{1,0:T(8,128)(2,1)S(1)} %get-tuple-element.13), channel_id=1, source_target_pairs={{0,1},{1,0},{2,3},{3,2},{4,5},{5,4},{6,7},{7,6},{8,9},{9,8},{10,11... | collective-permute-start | bytes 3145736 | tf_op jit(solution)/shard_map/ppermute | solution.py:11
  69.7 17.1 %copy-start.1 = (bf16[896,2048]{1,0:T(8,128)(2,1)S(1)}, bf16[896,2048]{1,0:T(8,128)(2,1)}, u32[]{:S(2)}) copy-start(bf16[896,2048]{1,0:T(8,128)(2,1)} %param.7) | copy-start | bytes 11010052
  88.1 2.7 %collective-permute-start.7 = (bf16[256,2048]{1,0:T(8,128)(2,1)S(1)}, bf16[256,2048]{1,0:T(8,128)(2,1)S(1)}, u32[]{:S(2)}, u32[]{:S(2)}) collective-permute-start(bf16[256,2048]{1,0:T(8,128)(2,1)S(1)} %convolution_convert_fusion), channel_id=1, source_target_pairs={{0,1},{1,0},{2,3},{3,2},{4,5},{5,4},{6,7},{7,6},{8,9},{9,8},{10,11... | collective-permute-start | bytes 3145736 | tf_op jit(solution)/shard_map/ppermute | solution.py:11
  92.1 9.6 %collective-permute-start.10 = (bf16[64,2048]{1,0:T(8,128)(2,1)S(1)}, bf16[64,2048]{1,0:T(8,128)(2,1)S(1)}, u32[]{:S(2)}, u32[]{:S(2)}) collective-permute-start(bf16[64,2048]{1,0:T(8,128)(2,1)S(1)} %get-tuple-element.6), channel_id=1, source_target_pairs={{0,24},{1,25},{2,26},{3,27},{4,28},{5,29},{6,30},{7,31},{8,16},{9,... | collective-permute-start | bytes 786440 | tf_op jit(solution)/shard_map/ppermute | solution.py:11
  92.5 9.3 %collective-permute-start.8 = (bf16[64,2048]{1,0:T(8,128)(2,1)S(1)}, bf16[64,2048]{1,0:T(8,128)(2,1)S(1)}, u32[]{:S(2)}, u32[]{:S(2)}) collective-permute-start(bf16[64,2048]{1,0:T(8,128)(2,1)S(1)} %get-tuple-element.5), channel_id=1, source_target_pairs={{0,8},{1,9},{2,10},{3,11},{4,12},{5,13},{6,14},{7,15},{8,0},{9,1},... | collective-permute-start | bytes 786440 | tf_op jit(solution)/shard_map/ppermute | solution.py:11
  92.5 16.1 %collective-permute-start.9 = (bf16[64,2048]{1,0:T(8,128)(2,1)S(1)}, bf16[64,2048]{1,0:T(8,128)(2,1)S(1)}, u32[]{:S(2)}, u32[]{:S(2)}) collective-permute-start(bf16[64,2048]{1,0:T(8,128)(2,1)S(1)} %get-tuple-element.7), channel_id=1, source_target_pairs={{0,16},{1,17},{2,18},{3,19},{4,20},{5,21},{6,22},{7,23},{8,24},{9,... | collective-permute-start | bytes 786440 | tf_op jit(solution)/shard_map/ppermute | solution.py:11
  108.7 6.7 %collective-permute-start.11 = (bf16[16,2048]{1,0:T(8,128)(2,1)S(1)}, bf16[16,2048]{1,0:T(8,128)(2,1)S(1)}, u32[]{:S(2)}, u32[]{:S(2)}) collective-permute-start(bf16[16,2048]{1,0:T(8,128)(2,1)S(1)} %get-tuple-element.10), channel_id=1, source_target_pairs={{0,2},{1,3},{2,0},{3,1},{4,6},{5,7},{6,4},{7,5},{8,10},{9,11},{10,... | collective-permute-start | bytes 196616 | tf_op jit(solution)/shard_map/ppermute | solution.py:11
  110.8 8.3 %collective-permute-start.12 = (bf16[16,2048]{1,0:T(8,128)(2,1)S(1)}, bf16[16,2048]{1,0:T(8,128)(2,1)S(1)}, u32[]{:S(2)}, u32[]{:S(2)}) collective-permute-start(bf16[16,2048]{1,0:T(8,128)(2,1)S(1)} %get-tuple-element.12), channel_id=1, source_target_pairs={{0,4},{1,5},{2,6},{3,7},{4,0},{5,1},{6,2},{7,3},{8,12},{9,13},{10,... | collective-permute-start | bytes 196616 | tf_op jit(solution)/shard_map/ppermute | solution.py:11
  115.4 6.5 %collective-permute-start.13 = (bf16[16,2048]{1,0:T(8,128)(2,1)S(1)}, bf16[16,2048]{1,0:T(8,128)(2,1)S(1)}, u32[]{:S(2)}, u32[]{:S(2)}) collective-permute-start(bf16[16,2048]{1,0:T(8,128)(2,1)S(1)} %get-tuple-element.11), channel_id=1, source_target_pairs={{0,6},{1,7},{2,4},{3,5},{4,2},{5,3},{6,0},{7,1},{8,14},{9,15},{10,... | collective-permute-start | bytes 196616 | tf_op jit(solution)/shard_map/ppermute | solution.py:11

commit v2 on v1

v2 whole, which is shorter than its diff:
```python
import jax
import jax.numpy as jnp
from jax import lax
from jax.sharding import PartitionSpec as P

CORES, Z_PARTS, Y_PARTS = 2, 4, 4
CHUNKS = 2


def swap(value, step):
    size = CORES * Z_PARTS * Y_PARTS
    return lax.ppermute(value, "gy", [(a, a ^ step) for a in range(size)])


def gather_steps(value, unit, parts):
    return jnp.concatenate([value] + [swap(value, unit * i) for i in range(1, parts)], 0)


def reduce_steps(value, unit, parts):
    rows = value.shape[0] // parts
    pieces = [value[i * rows:(i + 1) * rows] for i in range(parts)]
    total = pieces[0].astype(jnp.float32)
    for i in range(1, parts):
        total = total + swap(pieces[i], unit * i).astype(jnp.float32)
    return total.astype(jnp.bfloat16)


def after(value, *others):
    return lax.optimization_barrier((value,) + others)[0]


def dot(left, right):
    return jnp.dot(left, right, preferred_element_type=jnp.float32)


def per_device(tokens, gate_weight, up_weight, down_weight):
    width = gate_weight.shape[1]
    groups = lax.axis_size("gx")
    size = tokens.shape[0] // CHUNKS

    def project(part):
        part = gather_steps(part, 1, CORES)
        gate = dot(part, gate_weight).astype(jnp.bfloat16)
        up = dot(part, up_weight).astype(jnp.bfloat16)
        rows = part.shape[0] // groups
        return jnp.concatenate(
            [gate.reshape(groups, rows, width), up.reshape(groups, rows, width)], 2)

    def join(terms):
        summed = terms.astype(jnp.float32).sum(0)
        return (jax.nn.silu(summed[:, :width]) * summed[:, width:]).astype(jnp.bfloat16)

    def exchange(value):
        return lax.all_to_all(value, "gx", 0, 0)

    def spread(part):
        return exchange(jnp.broadcast_to(part[None], (groups,) + part.shape)).reshape(-1, width)

    def down(hidden):
        half = hidden.shape[0] // CORES
        came = swap(dot(hidden[half:], down_weight).astype(jnp.bfloat16), 1)
        mine = dot(hidden[:half], down_weight)
        return (mine + came.astype(jnp.float32)).astype(jnp.bfloat16)

    def over_z(value):
        return gather_steps(value, CORES, Z_PARTS)

    def over_y(value):
        return gather_steps(value, CORES * Z_PARTS, Y_PARTS)

    first, second = tokens[:size], tokens[size:]
    first = over_z(first)
    second = over_z(after(second, first))
    first = over_y(first)
    term_a = project(first)
    second = over_y(second)
    terms_a = exchange(term_a)
    hidden_a = join(terms_a)
    term_b = project(after(second, terms_a))
    all_a = spread(hidden_a)
    out_a = down(all_a)
    terms_b = exchange(after(term_b, all_a))
    out_a = reduce_steps(out_a, CORES * Z_PARTS, Y_PARTS)
    all_b = spread(join(terms_b))
    out_a = reduce_steps(out_a, CORES, Z_PARTS)
    out_b = down(all_b)
    out_b = reduce_steps(out_b, CORES * Z_PARTS, Y_PARTS)
    out_b = reduce_steps(out_b, CORES, Z_PARTS)
    return jnp.concatenate([out_a, out_b], 0)


def solution(mesh):
    in_specs = (P("gy", "gx"), P("gx", "gy"), P("gx", "gy"), P("gy", "gx"))
    out_specs = P("gy", "gx")
    return jax.shard_map(
        per_device, mesh=mesh, in_specs=in_specs, out_specs=out_specs, check_vma=False
    )
```

time: 124 us -> 140 us (1.13)
  starting transfers between devices: 25.2 us -> 69.8 us
  blocking collectives: 44.5 us -> 0 us
  matrix products: 8.54 us -> 18.6 us
  waiting for transfers between devices: 41.6 us -> 44.6 us
  other arithmetic: 1.12 us -> 3.26 us
    all_to_all x2 -> x0, blocking collectives: 44.5 us -> none  [the longest x1 27.7 us: per_device(): terms = lax.all_to_all(term.reshape(groups, rows, 2 * width), 'gx', 0, 0)]
    ppermute x14 -> x28, starting transfers between devices: 25.2 us -> 48.1 us  [swap(): return lax.ppermute(value, 'gy', [(a, a ^ step) for a in range(size)])]
    all_to_all x0 -> x4, starting transfers between devices: none -> 21.7 us  [exchange(): return lax.all_to_all(value, 'gx', 0, 0)]
    all_to_all x0 -> x4, waiting for transfers between devices: none -> 10.9 us  [exchange(): return lax.all_to_all(value, 'gx', 0, 0)]
    dot_general x3 -> x8, matrix products: 8.54 us -> 18.6 us  [dot(): return jnp.dot(left, right, preferred_element_type=jnp.float32)]
    ppermute x14 -> x28, waiting for transfers between devices: 41.6 us -> 33.7 us  [swap(): return lax.ppermute(value, 'gy', [(a, a ^ step) for a in range(size)])]
    concatenate x0 -> x4, other arithmetic: none -> 2.73 us  [the longest x2 2.09 us: project(): jnp.concatenate([gate.reshape(groups, rows, width), up.reshape(groups, ro...]
    broadcast_in_dim x1 -> x2, local copies, waits for them, and re-layouts: 0.12 us -> 1.63 us  [spread(): jnp.broadcast_to(part[None], (groups,) + part.shape)]
  transfers between devices with their start and end apart: 14 -> 32, of which waited for: 11 -> 17; matrix products, arithmetic and copies ran while one was open for 1% -> 16% of each run, Pallas kernels for 0% -> 0%
where the time goes in v2:
time: 140 us; the launch traced here: 139 us
  starting transfers between devices  69.8 us (50%)
  waiting for transfers between devices  44.6 us (32%)
  matrix products  18.6 us (13%)
  other arithmetic  3.26 us (2%)
  local copies, waits for them, and re-layouts  2.8 us (2%)
    ppermute x28, starting transfers between devices, swap(): return lax.ppermute(value, 'gy', [(a, a ^ step) for a in range(size)])  48.1 us
    ppermute x28, waiting for transfers between devices, swap(): return lax.ppermute(value, 'gy', [(a, a ^ step) for a in range(size)])  33.7 us
    all_to_all x4, starting transfers between devices, exchange(): return lax.all_to_all(value, 'gx', 0, 0)  21.7 us
    dot_general x8, matrix products, dot(): return jnp.dot(left, right, preferred_element_type=jnp.float32)  18.6 us
    all_to_all x4, waiting for transfers between devices, exchange(): return lax.all_to_all(value, 'gx', 0, 0)  10.9 us
  transfers between devices with their start and end apart: 32, of which 17 were waited for; matrix products, arithmetic and copies ran while one was open for 16% of the time, Pallas kernels for 0%

profile of v2, /device:TPU:2, one launch (start us, length us, event | category | flops | bytes accessed | tf_op | source)
XLA Modules:
  0.0 139.4 jit_solution(4422000336456340409)
XLA Ops:
  0.0 0.8 constant_dynamic-update-slice_fusion.6
  0.8 3.4 %collective-permute-start = (bf16[8,2048]{1,0:T(8,128)(2,1)S(1)}, bf16[8,2048]{1,0:T(8,128)(2,1)S(1)}, u32[]{:S(2)}, u32[]{:S(2)}) collective-permute-start(bf16[8,2048]{1,0:T(8,128)(2,1)S(1)} %get-tuple-element.34), channel_id=1, source_target_pairs={{0,2},{1,3},{2,0},{3,1},{4,6},{5,7},{6,4},{7,5},{8,10},{9,11},{10,... | collective-permute-start | bytes 98312 | tf_op jit(solution)/shard_map/ppermute | solution.py:12
  4.1 5.4 %collective-permute-start.1 = (bf16[8,2048]{1,0:T(8,128)(2,1)S(1)}, bf16[8,2048]{1,0:T(8,128)(2,1)S(1)}, u32[]{:S(2)}, u32[]{:S(2)}) collective-permute-start(bf16[8,2048]{1,0:T(8,128)(2,1)S(1)} %get-tuple-element.34), channel_id=1, source_target_pairs={{0,4},{1,5},{2,6},{3,7},{4,0},{5,1},{6,2},{7,3},{8,12},{9,13},{10,... | collective-permute-start | bytes 98312 | tf_op jit(solution)/shard_map/ppermute | solution.py:12
  9.5 2.4 %collective-permute-done.1 = bf16[8,2048]{1,0:T(8,128)(2,1)S(1)} collective-permute-done((bf16[8,2048]{1,0:T(8,128)(2,1)S(1)}, bf16[8,2048]{1,0:T(8,128)(2,1)S(1)}, u32[]{:S(2)}, u32[]{:S(2)}) %collective-permute-start.1) | collective-permute-done | bytes 32800 | tf_op jit(solution)/shard_map/ppermute | solution.py:12
  12.0 3.6 %collective-permute-done.2 = bf16[8,2048]{1,0:T(8,128)(2,1)S(1)} collective-permute-done((bf16[8,2048]{1,0:T(8,128)(2,1)S(1)}, bf16[8,2048]{1,0:T(8,128)(2,1)S(1)}, u32[]{:S(2)}, u32[]{:S(2)}) %collective-permute-start.2) | collective-permute-done | bytes 32800 | tf_op jit(solution)/shard_map/ppermute | solution.py:12
  15.6 1.7 %collective-permute-start.3 = (bf16[32,2048]{1,0:T(8,128)(2,1)S(1)}, bf16[32,2048]{1,0:T(8,128)(2,1)S(1)}, u32[]{:S(2)}, u32[]{:S(2)}) collective-permute-start(bf16[32,2048]{1,0:T(8,128)(2,1)S(1)} %pad_maximum_fusion.2), channel_id=1, source_target_pairs={{0,8},{1,9},{2,10},{3,11},{4,12},{5,13},{6,14},{7,15},{8,0},{9,1},... | collective-permute-start | bytes 393224 | tf_op jit(solution)/shard_map/ppermute | solution.py:12
  17.2 2.9 %collective-permute-start.4 = (bf16[32,2048]{1,0:T(8,128)(2,1)S(1)}, bf16[32,2048]{1,0:T(8,128)(2,1)S(1)}, u32[]{:S(2)}, u32[]{:S(2)}) collective-permute-start(bf16[32,2048]{1,0:T(8,128)(2,1)S(1)} %pad_maximum_fusion.2), channel_id=1, source_target_pairs={{0,16},{1,17},{2,18},{3,19},{4,20},{5,21},{6,22},{7,23},{8,24},{9,... | collective-permute-start | bytes 393224 | tf_op jit(solution)/shard_map/ppermute | solution.py:12
  20.1 0.2 collective-permute-start.5
  20.4 1.1 collective-permute-done.3
  21.5 3.0 %collective-permute-done.4 = bf16[32,2048]{1,0:T(8,128)(2,1)S(1)} collective-permute-done((bf16[32,2048]{1,0:T(8,128)(2,1)S(1)}, bf16[32,2048]{1,0:T(8,128)(2,1)S(1)}, u32[]{:S(2)}, u32[]{:S(2)}) %collective-permute-start.4) | collective-permute-done | bytes 131104 | tf_op jit(solution)/shard_map/ppermute | solution.py:12
  24.5 1.8 %collective-permute-done.5 = bf16[32,2048]{1,0:T(8,128)(2,1)S(1)} collective-permute-done((bf16[32,2048]{1,0:T(8,128)(2,1)S(1)}, bf16[32,2048]{1,0:T(8,128)(2,1)S(1)}, u32[]{:S(2)}, u32[]{:S(2)}) %collective-permute-start.5) | collective-permute-done | bytes 131104 | tf_op jit(solution)/shard_map/ppermute | solution.py:12
  26.3 0.1 collective-permute-start.6
  26.4 1.5 %collective-permute-start.14 = (bf16[8,2048]{1,0:T(8,128)(2,1)S(1)}, bf16[8,2048]{1,0:T(8,128)(2,1)S(1)}, u32[]{:S(2)}, u32[]{:S(2)}) collective-permute-start(bf16[8,2048]{1,0:T(8,128)(2,1)S(1)} %get-tuple-element.7), channel_id=1, source_target_pairs={{0,2},{1,3},{2,0},{3,1},{4,6},{5,7},{6,4},{7,5},{8,10},{9,11},{10,... | collective-permute-start | bytes 98312 | tf_op jit(solution)/shard_map/ppermute | solution.py:12
  28.0 0.4 collective-permute-done.6
  28.4 3.5 %convolution_convert_fusion.5 = bf16[256,896]{1,0:T(8,128)(2,1)S(1)} fusion(bf16[256,2048]{1,0:T(8,128)(2,1)S(1)} %constant_dynamic-update-slice_fusion.7, bf16[2048,896]{1,0:T(8,128)(2,1)} %param.5), kind=kOutput, calls=%fused_computation.7 | convolution fusion | flops 939753472 | bytes 5177344 | tf_op jit(solution)/shard_map/dot_general | solution.py:33
  31.9 1.3 convolution_convert_fusion.4
  33.1 1.0 pad_maximum_fusion
  34.2 5.3 %all-to-all-start = ((bf16[8,32,1792]{2,1,0:T(8,128)(2,1)}), bf16[8,32,1792]{2,1,0:T(8,128)(2,1)S(1)}, u32[]{:S(2)}, u32[]{:S(2)}) async-start(bf16[8,32,1792]{2,1,0:T(8,128)(2,1)} %pad_maximum_fusion), calls=%async_computation | async-start | bytes 1835008 | tf_op jit(solution)/shard_map/all_to_all | solution.py:54
  39.5 2.5 %collective-permute-start.15 = (bf16[8,2048]{1,0:T(8,128)(2,1)S(1)}, bf16[8,2048]{1,0:T(8,128)(2,1)S(1)}, u32[]{:S(2)}, u32[]{:S(2)}) collective-permute-start(bf16[8,2048]{1,0:T(8,128)(2,1)S(1)} %get-tuple-element.7), channel_id=1, source_target_pairs={{0,4},{1,5},{2,6},{3,7},{4,0},{5,1},{6,2},{7,3},{8,12},{9,13},{10,... | collective-permute-start | bytes 98312 | tf_op jit(solution)/shard_map/ppermute | solution.py:12
  42.0 2.6 %collective-permute-start.16 = (bf16[8,2048]{1,0:T(8,128)(2,1)S(1)}, bf16[8,2048]{1,0:T(8,128)(2,1)S(1)}, u32[]{:S(2)}, u32[]{:S(2)}) collective-permute-start(bf16[8,2048]{1,0:T(8,128)(2,1)S(1)} %get-tuple-element.7), channel_id=1, source_target_pairs={{0,6},{1,7},{2,4},{3,5},{4,2},{5,3},{6,0},{7,1},{8,14},{9,15},{10,... | collective-permute-start | bytes 98312 | tf_op jit(solution)/shard_map/ppermute | solution.py:12
  44.6 9.5 %collective-permute-done.15 = bf16[8,2048]{1,0:T(8,128)(2,1)S(1)} collective-permute-done((bf16[8,2048]{1,0:T(8,128)(2,1)S(1)}, bf16[8,2048]{1,0:T(8,128)(2,1)S(1)}, u32[]{:S(2)}, u32[]{:S(2)}) %collective-permute-start.15) | collective-permute-done | bytes 32800 | tf_op jit(solution)/shard_map/ppermute | solution.py:12
  54.1 0.1 collective-permute-start.17
  54.2 2.4 %collective-permute-start.18 = (bf16[32,2048]{1,0:T(8,128)(2,1)S(1)}, bf16[32,2048]{1,0:T(8,128)(2,1)S(1)}, u32[]{:S(2)}, u32[]{:S(2)}) collective-permute-start(bf16[32,2048]{1,0:T(8,128)(2,1)S(1)} %get-tuple-element.41), channel_id=1, source_target_pairs={{0,16},{1,17},{2,18},{3,19},{4,20},{5,21},{6,22},{7,23},{8,24},{9,... | collective-permute-start | bytes 393224 | tf_op jit(solution)/shard_map/ppermute | solution.py:12
  56.6 2.3 %collective-permute-start.19 = (bf16[32,2048]{1,0:T(8,128)(2,1)S(1)}, bf16[32,2048]{1,0:T(8,128)(2,1)S(1)}, u32[]{:S(2)}, u32[]{:S(2)}) collective-permute-start(bf16[32,2048]{1,0:T(8,128)(2,1)S(1)} %get-tuple-element.41), channel_id=1, source_target_pairs={{0,24},{1,25},{2,26},{3,27},{4,28},{5,29},{6,30},{7,31},{8,16},{9,... | collective-permute-start | bytes 393224 | tf_op jit(solution)/shard_map/ppermute | solution.py:12
  58.9 0.4 collective-permute-done.17
  59.4 1.8 %collective-permute-done.18 = bf16[32,2048]{1,0:T(8,128)(2,1)S(1)} collective-permute-done((bf16[32,2048]{1,0:T(8,128)(2,1)S(1)}, bf16[32,2048]{1,0:T(8,128)(2,1)S(1)}, u32[]{:S(2)}, u32[]{:S(2)}) %collective-permute-start.18) | collective-permute-done | bytes 131104 | tf_op jit(solution)/shard_map/ppermute | solution.py:12
  61.2 1.6 %collective-permute-done.19 = bf16[32,2048]{1,0:T(8,128)(2,1)S(1)} collective-permute-done((bf16[32,2048]{1,0:T(8,128)(2,1)S(1)}, bf16[32,2048]{1,0:T(8,128)(2,1)S(1)}, u32[]{:S(2)}, u32[]{:S(2)}) %collective-permute-start.19) | collective-permute-done | bytes 131104 | tf_op jit(solution)/shard_map/ppermute | solution.py:12
  62.8 0.1 collective-permute-start.20
  62.9 0.1 convert_reduce_fusion.1
  63.1 0.8 broadcast_in_dim.4
  63.9 5.4 %all-to-all-start.1 = ((bf16[8,32,896]{2,1,0:T(8,128)(2,1)}), bf16[8,32,896]{2,1,0:T(8,128)(2,1)S(1)}, u32[]{:S(2)}, u32[]{:S(2)}) async-start(bf16[8,32,896]{2,1,0:T(8,128)(2,1)} %broadcast_in_dim.4), calls=%async_computation.1 | async-start | bytes 917504 | tf_op jit(solution)/shard_map/all_to_all | solution.py:54
  69.4 3.5 %convolution_convert_fusion.3 = bf16[256,896]{1,0:T(8,128)(2,1)S(1)} fusion(bf16[256,2048]{1,0:T(8,128)(2,1)S(1)} %constant_dynamic-update-slice_fusion.26, bf16[2048,896]{1,0:T(8,128)(2,1)} %param.5), kind=kOutput, calls=%fused_computation.5 | convolution fusion | flops 939753472 | bytes 5177344 | tf_op jit(solution)/shard_map/dot_general | solution.py:33
  72.9 1.3 convolution_convert_fusion.2
  74.1 1.0 pad_maximum_fusion.1
  75.2 2.0 %all-to-all-done.1 = bf16[8,32,896]{2,1,0:T(8,128)(2,1)S(1)} async-done(((bf16[8,32,896]{2,1,0:T(8,128)(2,1)}), bf16[8,32,896]{2,1,0:T(8,128)(2,1)S(1)}, u32[]{:S(2)}, u32[]{:S(2)}) %all-to-all-start.1) | async-done | bytes 458784 | tf_op jit(solution)/shard_map/all_to_all | solution.py:54
  77.1 5.6 %all-to-all-start.2 = ((bf16[8,32,1792]{2,1,0:T(8,128)(2,1)}), bf16[8,32,1792]{2,1,0:T(8,128)(2,1)S(1)}, u32[]{:S(2)}, u32[]{:S(2)}) async-start(bf16[8,32,1792]{2,1,0:T(8,128)(2,1)} %pad_maximum_fusion.1), calls=%async_computation.2 | async-start | bytes 1835008 | tf_op jit(solution)/shard_map/all_to_all | solution.py:54
  82.8 2.8 %convolution_convert_fusion.1 = bf16[128,2048]{1,0:T(8,128)(2,1)S(1)} fusion(bf16[128,896]{1,0:T(8,128)(2,1)S(1)} %bitcast.26, bf16[896,2048]{1,0:T(8,128)(2,1)} %param.7), kind=kOutput, calls=%fused_computation.1 | convolution fusion | flops 470024192 | bytes 4423680 | tf_op jit(solution)/shard_map/dot_general | solution.py:33
  85.6 0.1 collective-permute-start.7
  85.7 8.9 %all-to-all-done.2 = bf16[8,32,1792]{2,1,0:T(8,128)(2,1)S(1)} async-done(((bf16[8,32,1792]{2,1,0:T(8,128)(2,1)}), bf16[8,32,1792]{2,1,0:T(8,128)(2,1)S(1)}, u32[]{:S(2)}, u32[]{:S(2)}) %all-to-all-start.2) | async-done | bytes 917536 | tf_op jit(solution)/shard_map/all_to_all | solution.py:54
  94.6 0.1 convert_reduce_fusion
  94.8 0.8 broadcast_in_dim.5
  95.6 5.5 %all-to-all-start.3 = ((bf16[8,32,896]{2,1,0:T(8,128)(2,1)}), bf16[8,32,896]{2,1,0:T(8,128)(2,1)S(1)}, u32[]{:S(2)}, u32[]{:S(2)}) async-start(bf16[8,32,896]{2,1,0:T(8,128)(2,1)} %broadcast_in_dim.5), calls=%async_computation.3 | async-start | bytes 917504 | tf_op jit(solution)/shard_map/all_to_all | solution.py:54
  101.0 2.8 %add_convert_fusion.1 = bf16[128,2048]{1,0:T(8,128)(2,1)S(1)} fusion(bf16[128,2048]{1,0:T(8,128)(2,1)S(1)} %collective-permute-done.7, bf16[128,896]{1,0:T(8,128)(2,1)S(1)} %bitcast.25, bf16[896,2048]{1,0:T(8,128)(2,1)} %param.7), kind=kOutput, calls=%fused_computation.9 | convolution fusion | flops 470548480 | bytes 4947968 | tf_op jit(solution)/shard_map/dot_general | solution.py:33
  103.8 2.3 %collective-permute-start.10 = (bf16[32,2048]{1,0:T(8,128)(2,1)S(1)}, bf16[32,2048]{1,0:T(8,128)(2,1)S(1)}, u32[]{:S(2)}, u32[]{:S(2)}) collective-permute-start(bf16[32,2048]{1,0:T(8,128)(2,1)S(1)} %get-tuple-element.10), channel_id=1, source_target_pairs={{0,24},{1,25},{2,26},{3,27},{4,28},{5,29},{6,30},{7,31},{8,16},{9,... | collective-permute-start | bytes 393224 | tf_op jit(solution)/shard_map/ppermute | solution.py:12
  106.2 2.4 %collective-permute-start.9 = (bf16[32,2048]{1,0:T(8,128)(2,1)S(1)}, bf16[32,2048]{1,0:T(8,128)(2,1)S(1)}, u32[]{:S(2)}, u32[]{:S(2)}) collective-permute-start(bf16[32,2048]{1,0:T(8,128)(2,1)S(1)} %get-tuple-element.11), channel_id=1, source_target_pairs={{0,16},{1,17},{2,18},{3,19},{4,20},{5,21},{6,22},{7,23},{8,24},{9,... | collective-permute-start | bytes 393224 | tf_op jit(solution)/shard_map/ppermute | solution.py:12
  108.7 2.9 %convolution_convert_fusion = bf16[128,2048]{1,0:T(8,128)(2,1)S(1)} fusion(bf16[128,896]{1,0:T(8,128)(2,1)S(1)} %bitcast.27, bf16[896,2048]{1,0:T(8,128)(2,1)} %param.7), kind=kOutput, calls=%fused_computation | convolution fusion | flops 470024192 | bytes 4423680 | tf_op jit(solution)/shard_map/dot_general | solution.py:33
  111.6 0.1 collective-permute-start.21
  111.7 1.2 collective-permute-done.9
  113.0 0.1 add_convert_fusion.3
  113.1 0.6 collective-permute-done.21
  113.6 0.7 add_convert_fusion
  114.4 1.2 collective-permute-start.22
  115.6 2.6 %collective-permute-start.23 = (bf16[32,2048]{1,0:T(8,128)(2,1)S(1)}, bf16[32,2048]{1,0:T(8,128)(2,1)S(1)}, u32[]{:S(2)}, u32[]{:S(2)}) collective-permute-start(bf16[32,2048]{1,0:T(8,128)(2,1)S(1)} %get-tuple-element.14), channel_id=1, source_target_pairs={{0,16},{1,17},{2,18},{3,19},{4,20},{5,21},{6,22},{7,23},{8,24},{9,... | collective-permute-start | bytes 393224 | tf_op jit(solution)/shard_map/ppermute | solution.py:12
  118.2 1.0 collective-permute-start.24
  119.2 1.5 %collective-permute-start.11 = (bf16[8,2048]{1,0:T(8,128)(2,1)S(1)}, bf16[8,2048]{1,0:T(8,128)(2,1)S(1)}, u32[]{:S(2)}, u32[]{:S(2)}) collective-permute-start(bf16[8,2048]{1,0:T(8,128)(2,1)S(1)} %get-tuple-element.19), channel_id=1, source_target_pairs={{0,2},{1,3},{2,0},{3,1},{4,6},{5,7},{6,4},{7,5},{8,10},{9,11},{10,... | collective-permute-start | bytes 98312 | tf_op jit(solution)/shard_map/ppermute | solution.py:12
  120.7 4.2 %collective-permute-start.12 = (bf16[8,2048]{1,0:T(8,128)(2,1)S(1)}, bf16[8,2048]{1,0:T(8,128)(2,1)S(1)}, u32[]{:S(2)}, u32[]{:S(2)}) collective-permute-start(bf16[8,2048]{1,0:T(8,128)(2,1)S(1)} %get-tuple-element.21), channel_id=1, source_target_pairs={{0,4},{1,5},{2,6},{3,7},{4,0},{5,1},{6,2},{7,3},{8,12},{9,13},{10,... | collective-permute-start | bytes 98312 | tf_op jit(solution)/shard_map/ppermute | solution.py:12
  124.9 0.9 collective-permute-start.13
  125.8 1.1 collective-permute-done.24
  126.9 1.5 %collective-permute-start.25 = (bf16[8,2048]{1,0:T(8,128)(2,1)S(1)}, bf16[8,2048]{1,0:T(8,128)(2,1)S(1)}, u32[]{:S(2)}, u32[]{:S(2)}) collective-permute-start(bf16[8,2048]{1,0:T(8,128)(2,1)S(1)} %get-tuple-element.22), channel_id=1, source_target_pairs={{0,2},{1,3},{2,0},{3,1},{4,6},{5,7},{6,4},{7,5},{8,10},{9,11},{10,... | collective-permute-start | bytes 98312 | tf_op jit(solution)/shard_map/ppermute | solution.py:12
  128.4 4.2 %collective-permute-start.26 = (bf16[8,2048]{1,0:T(8,128)(2,1)S(1)}, bf16[8,2048]{1,0:T(8,128)(2,1)S(1)}, u32[]{:S(2)}, u32[]{:S(2)}) collective-permute-start(bf16[8,2048]{1,0:T(8,128)(2,1)S(1)} %get-tuple-element.24), channel_id=1, source_target_pairs={{0,4},{1,5},{2,6},{3,7},{4,0},{5,1},{6,2},{7,3},{8,12},{9,13},{10,... | collective-permute-start | bytes 98312 | tf_op jit(solution)/shard_map/ppermute | solution.py:12
  132.7 0.9 collective-permute-start.27
  133.6 2.7 %collective-permute-done.26 = bf16[8,2048]{1,0:T(8,128)(2,1)S(1)} collective-permute-done((bf16[8,2048]{1,0:T(8,128)(2,1)S(1)}, bf16[8,2048]{1,0:T(8,128)(2,1)S(1)}, u32[]{:S(2)}, u32[]{:S(2)}) %collective-permute-start.26) | collective-permute-done | bytes 32800 | tf_op jit(solution)/shard_map/ppermute | solution.py:12
  136.3 2.4 %collective-permute-done.27 = bf16[8,2048]{1,0:T(8,128)(2,1)S(1)} collective-permute-done((bf16[8,2048]{1,0:T(8,128)(2,1)S(1)}, bf16[8,2048]{1,0:T(8,128)(2,1)S(1)}, u32[]{:S(2)}, u32[]{:S(2)}) %collective-permute-start.27) | collective-permute-done | bytes 32800 | tf_op jit(solution)/shard_map/ppermute | solution.py:12
  138.7 0.6 pad_maximum_fusion.3
  (51 shorter events, 0.6 us)
Async XLA Ops:
  0.8 8.8 %collective-permute-start = (bf16[8,2048]{1,0:T(8,128)(2,1)S(1)}, bf16[8,2048]{1,0:T(8,128)(2,1)S(1)}, u32[]{:S(2)}, u32[]{:S(2)}) collective-permute-start(bf16[8,2048]{1,0:T(8,128)(2,1)S(1)} %get-tuple-element.34), channel_id=1, source_target_pairs={{0,2},{1,3},{2,0},{3,1},{4,6},{5,7},{6,4},{7,5},{8,10},{9,11},{10,... | collective-permute-start | bytes 98312 | tf_op jit(solution)/shard_map/ppermute | solution.py:12
  4.1 7.8 %collective-permute-start.1 = (bf16[8,2048]{1,0:T(8,128)(2,1)S(1)}, bf16[8,2048]{1,0:T(8,128)(2,1)S(1)}, u32[]{:S(2)}, u32[]{:S(2)}) collective-permute-start(bf16[8,2048]{1,0:T(8,128)(2,1)S(1)} %get-tuple-element.34), channel_id=1, source_target_pairs={{0,4},{1,5},{2,6},{3,7},{4,0},{5,1},{6,2},{7,3},{8,12},{9,13},{10,... | collective-permute-start | bytes 98312 | tf_op jit(solution)/shard_map/ppermute | solution.py:12
  9.5 6.0 %collective-permute-start.2 = (bf16[8,2048]{1,0:T(8,128)(2,1)S(1)}, bf16[8,2048]{1,0:T(8,128)(2,1)S(1)}, u32[]{:S(2)}, u32[]{:S(2)}) collective-permute-start(bf16[8,2048]{1,0:T(8,128)(2,1)S(1)} %get-tuple-element.34), channel_id=1, source_target_pairs={{0,6},{1,7},{2,4},{3,5},{4,2},{5,3},{6,0},{7,1},{8,14},{9,15},{10,... | collective-permute-start | bytes 98312 | tf_op jit(solution)/shard_map/ppermute | solution.py:12
  15.6 5.9 %collective-permute-start.3 = (bf16[32,2048]{1,0:T(8,128)(2,1)S(1)}, bf16[32,2048]{1,0:T(8,128)(2,1)S(1)}, u32[]{:S(2)}, u32[]{:S(2)}) collective-permute-start(bf16[32,2048]{1,0:T(8,128)(2,1)S(1)} %pad_maximum_fusion.2), channel_id=1, source_target_pairs={{0,8},{1,9},{2,10},{3,11},{4,12},{5,13},{6,14},{7,15},{8,0},{9,1},... | collective-permute-start | bytes 393224 | tf_op jit(solution)/shard_map/ppermute | solution.py:12
  17.2 7.2 %collective-permute-start.4 = (bf16[32,2048]{1,0:T(8,128)(2,1)S(1)}, bf16[32,2048]{1,0:T(8,128)(2,1)S(1)}, u32[]{:S(2)}, u32[]{:S(2)}) collective-permute-start(bf16[32,2048]{1,0:T(8,128)(2,1)S(1)} %pad_maximum_fusion.2), channel_id=1, source_target_pairs={{0,16},{1,17},{2,18},{3,19},{4,20},{5,21},{6,22},{7,23},{8,24},{9,... | collective-permute-start | bytes 393224 | tf_op jit(solution)/shard_map/ppermute | solution.py:12
  20.1 6.2 %collective-permute-start.5 = (bf16[32,2048]{1,0:T(8,128)(2,1)S(1)}, bf16[32,2048]{1,0:T(8,128)(2,1)S(1)}, u32[]{:S(2)}, u32[]{:S(2)}) collective-permute-start(bf16[32,2048]{1,0:T(8,128)(2,1)S(1)} %pad_maximum_fusion.2), channel_id=1, source_target_pairs={{0,24},{1,25},{2,26},{3,27},{4,28},{5,29},{6,30},{7,31},{8,16},{9,... | collective-permute-start | bytes 393224 | tf_op jit(solution)/shard_map/ppermute | solution.py:12
  26.3 2.0 %collective-permute-start.6 = (bf16[128,2048]{1,0:T(8,128)(2,1)S(1)}, bf16[128,2048]{1,0:T(8,128)(2,1)S(1)}, u32[]{:S(2)}, u32[]{:S(2)}) collective-permute-start(bf16[128,2048]{1,0:T(8,128)(2,1)S(1)} %get-tuple-element.25), channel_id=1, source_target_pairs={{0,1},{1,0},{2,3},{3,2},{4,5},{5,4},{6,7},{7,6},{8,9},{9,8},{10,11... | collective-permute-start | bytes 1572872 | tf_op jit(solution)/shard_map/ppermute | solution.py:12
  26.4 18.1 %collective-permute-start.14 = (bf16[8,2048]{1,0:T(8,128)(2,1)S(1)}, bf16[8,2048]{1,0:T(8,128)(2,1)S(1)}, u32[]{:S(2)}, u32[]{:S(2)}) collective-permute-start(bf16[8,2048]{1,0:T(8,128)(2,1)S(1)} %get-tuple-element.7), channel_id=1, source_target_pairs={{0,2},{1,3},{2,0},{3,1},{4,6},{5,7},{6,4},{7,5},{8,10},{9,11},{10,... | collective-permute-start | bytes 98312 | tf_op jit(solution)/shard_map/ppermute | solution.py:12
  28.3 3.5 %copy-start.1 = (bf16[2048,896]{1,0:T(8,128)(2,1)S(1)}, bf16[2048,896]{1,0:T(8,128)(2,1)}, u32[]{:S(2)}) copy-start(bf16[2048,896]{1,0:T(8,128)(2,1)} %param.6) | copy-start | bytes 11010052
  34.2 28.7 %all-to-all-start = ((bf16[8,32,1792]{2,1,0:T(8,128)(2,1)}), bf16[8,32,1792]{2,1,0:T(8,128)(2,1)S(1)}, u32[]{:S(2)}, u32[]{:S(2)}) async-start(bf16[8,32,1792]{2,1,0:T(8,128)(2,1)} %pad_maximum_fusion), calls=%async_computation | async-start | bytes 1835008 | tf_op jit(solution)/shard_map/all_to_all | solution.py:54
  39.5 14.6 %collective-permute-start.15 = (bf16[8,2048]{1,0:T(8,128)(2,1)S(1)}, bf16[8,2048]{1,0:T(8,128)(2,1)S(1)}, u32[]{:S(2)}, u32[]{:S(2)}) collective-permute-start(bf16[8,2048]{1,0:T(8,128)(2,1)S(1)} %get-tuple-element.7), channel_id=1, source_target_pairs={{0,4},{1,5},{2,6},{3,7},{4,0},{5,1},{6,2},{7,3},{8,12},{9,13},{10,... | collective-permute-start | bytes 98312 | tf_op jit(solution)/shard_map/ppermute | solution.py:12
  42.0 12.1 %collective-permute-start.16 = (bf16[8,2048]{1,0:T(8,128)(2,1)S(1)}, bf16[8,2048]{1,0:T(8,128)(2,1)S(1)}, u32[]{:S(2)}, u32[]{:S(2)}) collective-permute-start(bf16[8,2048]{1,0:T(8,128)(2,1)S(1)} %get-tuple-element.7), channel_id=1, source_target_pairs={{0,6},{1,7},{2,4},{3,5},{4,2},{5,3},{6,0},{7,1},{8,14},{9,15},{10,... | collective-permute-start | bytes 98312 | tf_op jit(solution)/shard_map/ppermute | solution.py:12
  54.1 5.2 %collective-permute-start.17 = (bf16[32,2048]{1,0:T(8,128)(2,1)S(1)}, bf16[32,2048]{1,0:T(8,128)(2,1)S(1)}, u32[]{:S(2)}, u32[]{:S(2)}) collective-permute-start(bf16[32,2048]{1,0:T(8,128)(2,1)S(1)} %get-tuple-element.41), channel_id=1, source_target_pairs={{0,8},{1,9},{2,10},{3,11},{4,12},{5,13},{6,14},{7,15},{8,0},{9,1},... | collective-permute-start | bytes 393224 | tf_op jit(solution)/shard_map/ppermute | solution.py:12
  54.2 7.0 %collective-permute-start.18 = (bf16[32,2048]{1,0:T(8,128)(2,1)S(1)}, bf16[32,2048]{1,0:T(8,128)(2,1)S(1)}, u32[]{:S(2)}, u32[]{:S(2)}) collective-permute-start(bf16[32,2048]{1,0:T(8,128)(2,1)S(1)} %get-tuple-element.41), channel_id=1, source_target_pairs={{0,16},{1,17},{2,18},{3,19},{4,20},{5,21},{6,22},{7,23},{8,24},{9,... | collective-permute-start | bytes 393224 | tf_op jit(solution)/shard_map/ppermute | solution.py:12
  56.6 6.2 %collective-permute-start.19 = (bf16[32,2048]{1,0:T(8,128)(2,1)S(1)}, bf16[32,2048]{1,0:T(8,128)(2,1)S(1)}, u32[]{:S(2)}, u32[]{:S(2)}) collective-permute-start(bf16[32,2048]{1,0:T(8,128)(2,1)S(1)} %get-tuple-element.41), channel_id=1, source_target_pairs={{0,24},{1,25},{2,26},{3,27},{4,28},{5,29},{6,30},{7,31},{8,16},{9,... | collective-permute-start | bytes 393224 | tf_op jit(solution)/shard_map/ppermute | solution.py:12
  62.8 6.5 %collective-permute-start.20 = (bf16[128,2048]{1,0:T(8,128)(2,1)S(1)}, bf16[128,2048]{1,0:T(8,128)(2,1)S(1)}, u32[]{:S(2)}, u32[]{:S(2)}) collective-permute-start(bf16[128,2048]{1,0:T(8,128)(2,1)S(1)} %constant_dynamic-update-slice_fusion.19), channel_id=1, source_target_pairs={{0,1},{1,0},{2,3},{3,2},{4,5},{5,4},{6,7},{7,6},{8,9},{9,8},{10,11... | collective-permute-start | bytes 1572872 | tf_op jit(solution)/shard_map/ppermute | solution.py:12
  63.9 13.2 %all-to-all-start.1 = ((bf16[8,32,896]{2,1,0:T(8,128)(2,1)}), bf16[8,32,896]{2,1,0:T(8,128)(2,1)S(1)}, u32[]{:S(2)}, u32[]{:S(2)}) async-start(bf16[8,32,896]{2,1,0:T(8,128)(2,1)} %broadcast_in_dim.4), calls=%async_computation.1 | async-start | bytes 917504 | tf_op jit(solution)/shard_map/all_to_all | solution.py:54
  69.3 3.5 %copy-start.2 = (bf16[2048,896]{1,0:T(8,128)(2,1)S(1)}, bf16[2048,896]{1,0:T(8,128)(2,1)}, u32[]{:S(2)}) copy-start(bf16[2048,896]{1,0:T(8,128)(2,1)} %param.6) | copy-start | bytes 11010052
  77.1 17.4 %all-to-all-start.2 = ((bf16[8,32,1792]{2,1,0:T(8,128)(2,1)}), bf16[8,32,1792]{2,1,0:T(8,128)(2,1)S(1)}, u32[]{:S(2)}, u32[]{:S(2)}) async-start(bf16[8,32,1792]{2,1,0:T(8,128)(2,1)} %pad_maximum_fusion.1), calls=%async_computation.2 | async-start | bytes 1835008 | tf_op jit(solution)/shard_map/all_to_all | solution.py:54
  85.6 15.5 %collective-permute-start.7 = (bf16[128,2048]{1,0:T(8,128)(2,1)S(1)}, bf16[128,2048]{1,0:T(8,128)(2,1)S(1)}, u32[]{:S(2)}, u32[]{:S(2)}) collective-permute-start(bf16[128,2048]{1,0:T(8,128)(2,1)S(1)} %convolution_convert_fusion.1), channel_id=1, source_target_pairs={{0,1},{1,0},{2,3},{3,2},{4,5},{5,4},{6,7},{7,6},{8,9},{9,8},{10,11... | collective-permute-start | bytes 1572872 | tf_op jit(solution)/shard_map/ppermute | solution.py:12
  95.6 13.0 %all-to-all-start.3 = ((bf16[8,32,896]{2,1,0:T(8,128)(2,1)}), bf16[8,32,896]{2,1,0:T(8,128)(2,1)S(1)}, u32[]{:S(2)}, u32[]{:S(2)}) async-start(bf16[8,32,896]{2,1,0:T(8,128)(2,1)} %broadcast_in_dim.5), calls=%async_computation.3 | async-start | bytes 917504 | tf_op jit(solution)/shard_map/all_to_all | solution.py:54
  103.8 7.9 %collective-permute-start.10 = (bf16[32,2048]{1,0:T(8,128)(2,1)S(1)}, bf16[32,2048]{1,0:T(8,128)(2,1)S(1)}, u32[]{:S(2)}, u32[]{:S(2)}) collective-permute-start(bf16[32,2048]{1,0:T(8,128)(2,1)S(1)} %get-tuple-element.10), channel_id=1, source_target_pairs={{0,24},{1,25},{2,26},{3,27},{4,28},{5,29},{6,30},{7,31},{8,16},{9,... | collective-permute-start | bytes 393224 | tf_op jit(solution)/shard_map/ppermute | solution.py:12
  106.2 5.5 %collective-permute-start.8 = (bf16[32,2048]{1,0:T(8,128)(2,1)S(1)}, bf16[32,2048]{1,0:T(8,128)(2,1)S(1)}, u32[]{:S(2)}, u32[]{:S(2)}) collective-permute-start(bf16[32,2048]{1,0:T(8,128)(2,1)S(1)} %get-tuple-element.9), channel_id=1, source_target_pairs={{0,8},{1,9},{2,10},{3,11},{4,12},{5,13},{6,14},{7,15},{8,0},{9,1},... | collective-permute-start | bytes 393224 | tf_op jit(solution)/shard_map/ppermute | solution.py:12
  106.2 6.8 %collective-permute-start.9 = (bf16[32,2048]{1,0:T(8,128)(2,1)S(1)}, bf16[32,2048]{1,0:T(8,128)(2,1)S(1)}, u32[]{:S(2)}, u32[]{:S(2)}) collective-permute-start(bf16[32,2048]{1,0:T(8,128)(2,1)S(1)} %get-tuple-element.11), channel_id=1, source_target_pairs={{0,16},{1,17},{2,18},{3,19},{4,20},{5,21},{6,22},{7,23},{8,24},{9,... | collective-permute-start | bytes 393224 | tf_op jit(solution)/shard_map/ppermute | solution.py:12
  108.6 5.0 %copy-start = (bf16[896,2048]{1,0:T(8,128)(2,1)S(1)}, bf16[896,2048]{1,0:T(8,128)(2,1)}, u32[]{:S(2)}) copy-start(bf16[896,2048]{1,0:T(8,128)(2,1)} %param.7) | copy-start | bytes 11010052
  111.6 2.0 %collective-permute-start.21 = (bf16[128,2048]{1,0:T(8,128)(2,1)S(1)}, bf16[128,2048]{1,0:T(8,128)(2,1)S(1)}, u32[]{:S(2)}, u32[]{:S(2)}) collective-permute-start(bf16[128,2048]{1,0:T(8,128)(2,1)S(1)} %convolution_convert_fusion), channel_id=1, source_target_pairs={{0,1},{1,0},{2,3},{3,2},{4,5},{5,4},{6,7},{7,6},{8,9},{9,8},{10,11... | collective-permute-start | bytes 1572872 | tf_op jit(solution)/shard_map/ppermute | solution.py:12
  114.4 10.5 %collective-permute-start.22 = (bf16[32,2048]{1,0:T(8,128)(2,1)S(1)}, bf16[32,2048]{1,0:T(8,128)(2,1)S(1)}, u32[]{:S(2)}, u32[]{:S(2)}) collective-permute-start(bf16[32,2048]{1,0:T(8,128)(2,1)S(1)} %get-tuple-element.12), channel_id=1, source_target_pairs={{0,8},{1,9},{2,10},{3,11},{4,12},{5,13},{6,14},{7,15},{8,0},{9,1},... | collective-permute-start | bytes 393224 | tf_op jit(solution)/shard_map/ppermute | solution.py:12
  115.6 10.1 %collective-permute-start.23 = (bf16[32,2048]{1,0:T(8,128)(2,1)S(1)}, bf16[32,2048]{1,0:T(8,128)(2,1)S(1)}, u32[]{:S(2)}, u32[]{:S(2)}) collective-permute-start(bf16[32,2048]{1,0:T(8,128)(2,1)S(1)} %get-tuple-element.14), channel_id=1, source_target_pairs={{0,16},{1,17},{2,18},{3,19},{4,20},{5,21},{6,22},{7,23},{8,24},{9,... | collective-permute-start | bytes 393224 | tf_op jit(solution)/shard_map/ppermute | solution.py:12
  118.2 8.7 %collective-permute-start.24 = (bf16[32,2048]{1,0:T(8,128)(2,1)S(1)}, bf16[32,2048]{1,0:T(8,128)(2,1)S(1)}, u32[]{:S(2)}, u32[]{:S(2)}) collective-permute-start(bf16[32,2048]{1,0:T(8,128)(2,1)S(1)} %get-tuple-element.13), channel_id=1, source_target_pairs={{0,24},{1,25},{2,26},{3,27},{4,28},{5,29},{6,30},{7,31},{8,16},{9,... | collective-permute-start | bytes 393224 | tf_op jit(solution)/shard_map/ppermute | solution.py:12
  119.2 13.5 %collective-permute-start.11 = (bf16[8,2048]{1,0:T(8,128)(2,1)S(1)}, bf16[8,2048]{1,0:T(8,128)(2,1)S(1)}, u32[]{:S(2)}, u32[]{:S(2)}) collective-permute-start(bf16[8,2048]{1,0:T(8,128)(2,1)S(1)} %get-tuple-element.19), channel_id=1, source_target_pairs={{0,2},{1,3},{2,0},{3,1},{4,6},{5,7},{6,4},{7,5},{8,10},{9,11},{10,... | collective-permute-start | bytes 98312 | tf_op jit(solution)/shard_map/ppermute | solution.py:12
  120.7 12.9 %collective-permute-start.12 = (bf16[8,2048]{1,0:T(8,128)(2,1)S(1)}, bf16[8,2048]{1,0:T(8,128)(2,1)S(1)}, u32[]{:S(2)}, u32[]{:S(2)}) collective-permute-start(bf16[8,2048]{1,0:T(8,128)(2,1)S(1)} %get-tuple-element.21), channel_id=1, source_target_pairs={{0,4},{1,5},{2,6},{3,7},{4,0},{5,1},{6,2},{7,3},{8,12},{9,13},{10,... | collective-permute-start | bytes 98312 | tf_op jit(solution)/shard_map/ppermute | solution.py:12
  124.9 8.7 %collective-permute-start.13 = (bf16[8,2048]{1,0:T(8,128)(2,1)S(1)}, bf16[8,2048]{1,0:T(8,128)(2,1)S(1)}, u32[]{:S(2)}, u32[]{:S(2)}) collective-permute-start(bf16[8,2048]{1,0:T(8,128)(2,1)S(1)} %get-tuple-element.20), channel_id=1, source_target_pairs={{0,6},{1,7},{2,4},{3,5},{4,2},{5,3},{6,0},{7,1},{8,14},{9,15},{10,... | collective-permute-start | bytes 98312 | tf_op jit(solution)/shard_map/ppermute | solution.py:12
  126.9 6.6 %collective-permute-start.25 = (bf16[8,2048]{1,0:T(8,128)(2,1)S(1)}, bf16[8,2048]{1,0:T(8,128)(2,1)S(1)}, u32[]{:S(2)}, u32[]{:S(2)}) collective-permute-start(bf16[8,2048]{1,0:T(8,128)(2,1)S(1)} %get-tuple-element.22), channel_id=1, source_target_pairs={{0,2},{1,3},{2,0},{3,1},{4,6},{5,7},{6,4},{7,5},{8,10},{9,11},{10,... | collective-permute-start | bytes 98312 | tf_op jit(solution)/shard_map/ppermute | solution.py:12
  128.4 7.8 %collective-permute-start.26 = (bf16[8,2048]{1,0:T(8,128)(2,1)S(1)}, bf16[8,2048]{1,0:T(8,128)(2,1)S(1)}, u32[]{:S(2)}, u32[]{:S(2)}) collective-permute-start(bf16[8,2048]{1,0:T(8,128)(2,1)S(1)} %get-tuple-element.24), channel_id=1, source_target_pairs={{0,4},{1,5},{2,6},{3,7},{4,0},{5,1},{6,2},{7,3},{8,12},{9,13},{10,... | collective-permute-start | bytes 98312 | tf_op jit(solution)/shard_map/ppermute | solution.py:12
  132.7 6.1 %collective-permute-start.27 = (bf16[8,2048]{1,0:T(8,128)(2,1)S(1)}, bf16[8,2048]{1,0:T(8,128)(2,1)S(1)}, u32[]{:S(2)}, u32[]{:S(2)}) collective-permute-start(bf16[8,2048]{1,0:T(8,128)(2,1)S(1)} %get-tuple-element.23), channel_id=1, source_target_pairs={{0,6},{1,7},{2,4},{3,5},{4,2},{5,3},{6,0},{7,1},{8,14},{9,15},{10,... | collective-permute-start | bytes 98312 | tf_op jit(solution)/shard_map/ppermute | solution.py:12

commit v3 on v1

v3 whole, which is shorter than its diff:
```python
import jax
import jax.numpy as jnp
from jax import lax
from jax.sharding import PartitionSpec as P

CORES, Z_PARTS, Y_PARTS = 2, 4, 4


def swap(value, step):
    size = CORES * Z_PARTS * Y_PARTS
    return lax.ppermute(value, "gy", [(a, a ^ step) for a in range(size)])


def gather_core(value):
    return jnp.concatenate([value, swap(value, 1)], 0)


def gather_ring(value, unit):
    half = value.shape[0] // 2
    left, right = swap(value, unit), swap(value, unit * 3)
    across = [swap(right[:half], unit), swap(left[half:], unit * 3)]
    return jnp.concatenate([value, left] + across + [right], 0)


def add(*values):
    return sum(value.astype(jnp.float32) for value in values).astype(jnp.bfloat16)


def reduce_ring(value, unit):
    rows = value.shape[0] // 4
    half = rows // 2
    mine, left, across, right = (value[i * rows:(i + 1) * rows] for i in range(4))
    for_right = swap(across[:half], unit)
    for_left = swap(across[half:], unit * 3)
    left = jnp.concatenate([left[:half], add(left[half:], for_left)], 0)
    right = jnp.concatenate([add(right[:half], for_right), right[half:]], 0)
    return add(mine, swap(left, unit), swap(right, unit * 3))


def per_device(tokens, gate_weight, up_weight, down_weight):
    width = gate_weight.shape[1]
    groups = lax.axis_size("gx")
    both = jnp.concatenate([gate_weight, up_weight], 1)
    part = gather_ring(tokens, CORES)
    part = gather_ring(part, CORES * Z_PARTS)
    part = gather_core(part)
    term = jnp.dot(part, both, preferred_element_type=jnp.float32).astype(jnp.bfloat16)
    rows = term.shape[0] // groups
    terms = lax.all_to_all(term.reshape(groups, rows, 2 * width), "gx", 0, 0)
    summed = terms.astype(jnp.float32).sum(0)
    hidden_part = (jax.nn.silu(summed[:, :width]) * summed[:, width:]).astype(jnp.bfloat16)
    hidden = lax.all_to_all(
        jnp.broadcast_to(hidden_part[None], (groups, rows, width)), "gx", 0, 0
    ).reshape(groups * rows, width)
    half = hidden.shape[0] // 2
    theirs = jnp.dot(hidden[half:], down_weight, preferred_element_type=jnp.float32).astype(jnp.bfloat16)
    came = swap(theirs, 1)
    mine = lax.optimization_barrier(
        jnp.dot(hidden[:half], down_weight, preferred_element_type=jnp.float32))
    out = (mine + came.astype(jnp.float32)).astype(jnp.bfloat16)
    out = reduce_ring(out, CORES * Z_PARTS)
    return reduce_ring(out, CORES)


def solution(mesh):
    in_specs = (P("gy", "gx"), P("gx", "gy"), P("gx", "gy"), P("gy", "gx"))
    out_specs = P("gy", "gx")
    return jax.shard_map(
        per_device, mesh=mesh, in_specs=in_specs, out_specs=out_specs, check_vma=False
    )
```

time: 124 us -> 128 us (1.032)
  waiting for transfers between devices: 41.6 us -> 44.1 us
  starting transfers between devices: 25.2 us -> 26.8 us
    ppermute x14 -> x18, waiting for transfers between devices: 41.6 us -> 44.1 us  [swap(): return lax.ppermute(value, 'gy', [(a, a ^ step) for a in range(size)])]
    ppermute x14 -> x18, starting transfers between devices: 25.2 us -> 26.8 us  [swap(): return lax.ppermute(value, 'gy', [(a, a ^ step) for a in range(size)])]
  transfers between devices with their start and end apart: 14 -> 18, of which waited for: 11 -> 15; matrix products, arithmetic and copies ran while one was open for 1% -> 2% of each run, Pallas kernels for 0% -> 0%
where the time goes in v3:
time: 128 us; the launch traced here: 127 us
  blocking collectives  44.5 us (35%)
  waiting for transfers between devices  44.1 us (34%)
  starting transfers between devices  26.8 us (21%)
  matrix products  8.64 us (7%)
  other arithmetic  1.5 us (1%)
  local copies, waits for them, and re-layouts  1.41 us (1%)
    ppermute x18, waiting for transfers between devices, swap(): return lax.ppermute(value, 'gy', [(a, a ^ step) for a in range(size)])  44.1 us
    all_to_all x1, blocking collectives, per_device(): terms = lax.all_to_all(term.reshape(groups, rows, 2 * width), 'gx', 0, 0)  27.7 us
    ppermute x18, starting transfers between devices, swap(): return lax.ppermute(value, 'gy', [(a, a ^ step) for a in range(size)])  26.8 us
    all_to_all x1, blocking collectives, per_device(): lax.all_to_all(jnp.broadcast_to(hidden_part[None], (groups, rows, width))...  16.8 us
    dot_general x1, matrix products, per_device(): jnp.dot(part, both, preferred_element_type=jnp.float32).astype(jnp.bfloat16)  6.03 us
  transfers between devices with their start and end apart: 18, of which 15 were waited for; matrix products, arithmetic and copies ran while one was open for 2% of the time, Pallas kernels for 0%

profile of v3, /device:TPU:2, one launch (start us, length us, event | category | flops | bytes accessed | tf_op | source)
XLA Modules:
  0.0 127.2 jit_solution(4470084741584019062)
XLA Ops:
  0.0 3.3 %collective-permute-start = (bf16[16,2048]{1,0:T(8,128)(2,1)}, bf16[16,2048]{1,0:T(8,128)(2,1)S(1)}, u32[]{:S(2)}, u32[]{:S(2)}) collective-permute-start(bf16[16,2048]{1,0:T(8,128)(2,1)} %param.4), channel_id=1, source_target_pairs={{0,2},{1,3},{2,0},{3,1},{4,6},{5,7},{6,4},{7,5},{8,10},{9,11},{10,... | collective-permute-start | bytes 196616 | tf_op jit(solution)/shard_map/ppermute | solution.py:11
  3.3 4.5 %collective-permute-start.1 = (bf16[16,2048]{1,0:T(8,128)(2,1)}, bf16[16,2048]{1,0:T(8,128)(2,1)S(1)}, u32[]{:S(2)}, u32[]{:S(2)}) collective-permute-start(bf16[16,2048]{1,0:T(8,128)(2,1)} %param.4), channel_id=1, source_target_pairs={{0,6},{1,7},{2,4},{3,5},{4,2},{5,3},{6,0},{7,1},{8,14},{9,15},{10,... | collective-permute-start | bytes 196616 | tf_op jit(solution)/shard_map/ppermute | solution.py:11
  7.8 0.9 constant_dynamic-update-slice_fusion.13
  8.6 2.0 %collective-permute-done.1 = bf16[16,2048]{1,0:T(8,128)(2,1)S(1)} collective-permute-done((bf16[16,2048]{1,0:T(8,128)(2,1)}, bf16[16,2048]{1,0:T(8,128)(2,1)S(1)}, u32[]{:S(2)}, u32[]{:S(2)}) %collective-permute-start.1) | collective-permute-done | bytes 65568 | tf_op jit(solution)/shard_map/ppermute | solution.py:11
  10.7 2.0 %collective-permute-start.2 = (bf16[8,2048]{1,0:T(8,128)(2,1)S(1)}, bf16[8,2048]{1,0:T(8,128)(2,1)S(1)}, u32[]{:S(2)}, u32[]{:S(2)}) collective-permute-start(bf16[8,2048]{1,0:T(8,128)(2,1)S(1)} %slice.114), channel_id=1, source_target_pairs={{0,2},{1,3},{2,0},{3,1},{4,6},{5,7},{6,4},{7,5},{8,10},{9,11},{10,... | collective-permute-start | bytes 98312 | tf_op jit(solution)/shard_map/ppermute | solution.py:11
  12.7 0.0 collective-permute-done
  12.7 3.1 %collective-permute-start.3 = (bf16[8,2048]{1,0:T(8,128)(2,1)S(1)}, bf16[8,2048]{1,0:T(8,128)(2,1)S(1)}, u32[]{:S(2)}, u32[]{:S(2)}) collective-permute-start(bf16[8,2048]{1,0:T(8,128)(2,1)S(1)} %slice.115), channel_id=1, source_target_pairs={{0,6},{1,7},{2,4},{3,5},{4,2},{5,3},{6,0},{7,1},{8,14},{9,15},{10,... | collective-permute-start | bytes 98312 | tf_op jit(solution)/shard_map/ppermute | solution.py:11
  15.8 0.0 collective-permute-done.2
  15.9 2.9 %collective-permute-done.3 = bf16[8,2048]{1,0:T(8,128)(2,1)S(1)} collective-permute-done((bf16[8,2048]{1,0:T(8,128)(2,1)S(1)}, bf16[8,2048]{1,0:T(8,128)(2,1)S(1)}, u32[]{:S(2)}, u32[]{:S(2)}) %collective-permute-start.3) | collective-permute-done | bytes 32800 | tf_op jit(solution)/shard_map/ppermute | solution.py:11
  18.8 3.1 %collective-permute-start.5 = (bf16[64,2048]{1,0:T(8,128)(2,1)S(1)}, bf16[64,2048]{1,0:T(8,128)(2,1)S(1)}, u32[]{:S(2)}, u32[]{:S(2)}) collective-permute-start(bf16[64,2048]{1,0:T(8,128)(2,1)S(1)} %get-tuple-element.29), channel_id=1, source_target_pairs={{0,24},{1,25},{2,26},{3,27},{4,28},{5,29},{6,30},{7,31},{8,16},{9,... | collective-permute-start | bytes 786440 | tf_op jit(solution)/shard_map/ppermute | solution.py:11
  21.9 0.1 collective-permute-start.4
  22.0 4.4 %collective-permute-done.5 = bf16[64,2048]{1,0:T(8,128)(2,1)S(1)} collective-permute-done((bf16[64,2048]{1,0:T(8,128)(2,1)S(1)}, bf16[64,2048]{1,0:T(8,128)(2,1)S(1)}, u32[]{:S(2)}, u32[]{:S(2)}) %collective-permute-start.5) | collective-permute-done | bytes 262176 | tf_op jit(solution)/shard_map/ppermute | solution.py:11
  26.4 0.5 collective-permute-start.6
  26.9 2.5 %collective-permute-done.4 = bf16[64,2048]{1,0:T(8,128)(2,1)S(1)} collective-permute-done((bf16[64,2048]{1,0:T(8,128)(2,1)S(1)}, bf16[64,2048]{1,0:T(8,128)(2,1)S(1)}, u32[]{:S(2)}, u32[]{:S(2)}) %collective-permute-start.4) | collective-permute-done | bytes 262176 | tf_op jit(solution)/shard_map/ppermute | solution.py:11
  29.4 0.3 collective-permute-start.7
  29.7 0.0 copy-start.1
  29.7 1.8 %collective-permute-done.6 = bf16[32,2048]{1,0:T(8,128)(2,1)S(1)} collective-permute-done((bf16[32,2048]{1,0:T(8,128)(2,1)S(1)}, bf16[32,2048]{1,0:T(8,128)(2,1)S(1)}, u32[]{:S(2)}, u32[]{:S(2)}) %collective-permute-start.6) | collective-permute-done | bytes 131104 | tf_op jit(solution)/shard_map/ppermute | solution.py:11
  31.5 4.2 %collective-permute-done.7 = bf16[32,2048]{1,0:T(8,128)(2,1)S(1)} collective-permute-done((bf16[32,2048]{1,0:T(8,128)(2,1)S(1)}, bf16[32,2048]{1,0:T(8,128)(2,1)S(1)}, u32[]{:S(2)}, u32[]{:S(2)}) %collective-permute-start.7) | collective-permute-done | bytes 131104 | tf_op jit(solution)/shard_map/ppermute | solution.py:11
  35.7 0.1 collective-permute-start.8
  35.8 2.6 %collective-permute-done.8 = bf16[256,2048]{1,0:T(8,128)(2,1)S(1)} collective-permute-done((bf16[256,2048]{1,0:T(8,128)(2,1)S(1)}, bf16[256,2048]{1,0:T(8,128)(2,1)S(1)}, u32[]{:S(2)}, u32[]{:S(2)}) %collective-permute-start.8) | collective-permute-done | bytes 1048608 | tf_op jit(solution)/shard_map/ppermute | solution.py:11
  38.5 0.1 constant_dynamic-update-slice_fusion.14
  38.6 0.0 copy-done.1
  38.6 6.0 %fusion.4 = bf16[512,1792]{1,0:T(8,128)(2,1)S(1)} fusion(bf16[512,2048]{1,0:T(8,128)(2,1)S(1)} %constant_dynamic-update-slice_fusion.14, bf16[2048,896]{1,0:T(8,128)(2,1)S(1)} %copy-done.1, bf16[2048,896]{1,0:T(8,128)(2,1)} %param.5), kind=kOutput, calls=%fused_computation.5 | convolution fusion | flops 3773693952 | bytes 11272192 | tf_op jit(solution)/shard_map/dot_general | solution.py:47
  44.6 27.7 %all_to_all.10 = bf16[8,64,1792]{2,1,0:T(8,128)(2,1)S(1)} all-to-all(bf16[8,64,1792]{2,1,0:T(8,128)(2,1)S(1)} %bitcast.9), channel_id=1, replica_groups=mesh['gx'=8,'gy'=32] {'gx'}, dimensions={0} | all-to-all | bytes 3670016 | tf_op jit(solution)/shard_map/all_to_all | solution.py:49
  72.3 0.2 convert_reduce_fusion
  72.5 0.1 fusion.7
  72.6 0.0 copy-start
  72.6 0.1 broadcast_in_dim.2
  72.8 16.8 %all_to_all.11 = bf16[8,64,896]{2,1,0:T(8,128)(2,1)S(1)} all-to-all(bf16[8,64,896]{2,1,0:T(8,128)(2,1)S(1)} %broadcast_in_dim.2), channel_id=1, replica_groups=mesh['gx'=8,'gy'=32] {'gx'}, dimensions={0} | all-to-all | bytes 1835008 | tf_op jit(solution)/shard_map/all_to_all | solution.py:52
  89.6 0.1 fusion.10
  89.7 0.0 copy-done
  89.7 1.3 %convolution_convert_fusion = bf16[256,2048]{1,0:T(8,128)(2,1)S(1)} fusion(bf16[256,896]{1,0:T(8,128)(2,1)S(1)} %bitcast.10, bf16[896,2048]{1,0:T(8,128)(2,1)S(1)} %copy-done), kind=kOutput, calls=%fused_computation.6 | convolution fusion | flops 940048384 | bytes 5177344 | tf_op jit(solution)/shard_map/dot_general | solution.py:56
  91.0 0.1 collective-permute-start.9
  91.1 1.3 %fusion.12 = f32[256,2048]{1,0:T(8,128)S(1)} fusion(bf16[256,896]{1,0:T(8,128)(2,1)S(1)} %bitcast.8, bf16[896,2048]{1,0:T(8,128)(2,1)S(1)} %copy-done), kind=kOutput, calls=%fused_computation.48 | convolution fusion | flops 939524096 | bytes 6225920 | tf_op jit(solution)/shard_map/dot_general | solution.py:59
  92.4 1.3 %collective-permute-done.9 = bf16[256,2048]{1,0:T(8,128)(2,1)S(1)} collective-permute-done((bf16[256,2048]{1,0:T(8,128)(2,1)S(1)}, bf16[256,2048]{1,0:T(8,128)(2,1)S(1)}, u32[]{:S(2)}, u32[]{:S(2)}) %collective-permute-start.9) | collective-permute-done | bytes 1048608 | tf_op jit(solution)/shard_map/ppermute | solution.py:11
  93.8 0.3 add_convert_fusion
  94.1 0.3 collective-permute-start.10
  94.4 0.1 collective-permute-start.12
  94.5 6.6 %collective-permute-done.10 = bf16[32,2048]{1,0:T(8,128)(2,1)S(1)} collective-permute-done((bf16[32,2048]{1,0:T(8,128)(2,1)S(1)}, bf16[32,2048]{1,0:T(8,128)(2,1)S(1)}, u32[]{:S(2)}, u32[]{:S(2)}) %collective-permute-start.10) | collective-permute-done | bytes 131104 | tf_op jit(solution)/shard_map/ppermute | solution.py:11
  101.1 0.0 collective-permute-done.12
  101.1 0.1 add_convert_fusion.3
  101.2 0.1 collective-permute-start.11
  101.4 2.1 %collective-permute-start.13 = (bf16[64,2048]{1,0:T(8,128)(2,1)S(1)}, bf16[64,2048]{1,0:T(8,128)(2,1)S(1)}, u32[]{:S(2)}, u32[]{:S(2)}) collective-permute-start(bf16[64,2048]{1,0:T(8,128)(2,1)S(1)} %pad_maximum_fusion.1), channel_id=1, source_target_pairs={{0,24},{1,25},{2,26},{3,27},{4,28},{5,29},{6,30},{7,31},{8,16},{9,... | collective-permute-start | bytes 786440 | tf_op jit(solution)/shard_map/ppermute | solution.py:11
  103.4 5.4 %collective-permute-done.11 = bf16[64,2048]{1,0:T(8,128)(2,1)S(1)} collective-permute-done((bf16[64,2048]{1,0:T(8,128)(2,1)S(1)}, bf16[64,2048]{1,0:T(8,128)(2,1)S(1)}, u32[]{:S(2)}, u32[]{:S(2)}) %collective-permute-start.11) | collective-permute-done | bytes 262176 | tf_op jit(solution)/shard_map/ppermute | solution.py:11
  108.8 1.3 %collective-permute-done.13 = bf16[64,2048]{1,0:T(8,128)(2,1)S(1)} collective-permute-done((bf16[64,2048]{1,0:T(8,128)(2,1)S(1)}, bf16[64,2048]{1,0:T(8,128)(2,1)S(1)}, u32[]{:S(2)}, u32[]{:S(2)}) %collective-permute-start.13) | collective-permute-done | bytes 262176 | tf_op jit(solution)/shard_map/ppermute | solution.py:11
  110.2 0.1 add_convert_fusion.1
  110.3 3.8 %collective-permute-start.14 = (bf16[8,2048]{1,0:T(8,128)(2,1)S(1)}, bf16[8,2048]{1,0:T(8,128)(2,1)S(1)}, u32[]{:S(2)}, u32[]{:S(2)}) collective-permute-start(bf16[8,2048]{1,0:T(8,128)(2,1)S(1)} %get-tuple-element.16), channel_id=1, source_target_pairs={{0,6},{1,7},{2,4},{3,5},{4,2},{5,3},{6,0},{7,1},{8,14},{9,15},{10,... | collective-permute-start | bytes 98312 | tf_op jit(solution)/shard_map/ppermute | solution.py:11
  114.1 1.0 collective-permute-start.16
  115.1 1.3 %collective-permute-done.14 = bf16[8,2048]{1,0:T(8,128)(2,1)S(1)} collective-permute-done((bf16[8,2048]{1,0:T(8,128)(2,1)S(1)}, bf16[8,2048]{1,0:T(8,128)(2,1)S(1)}, u32[]{:S(2)}, u32[]{:S(2)}) %collective-permute-start.14) | collective-permute-done | bytes 32800 | tf_op jit(solution)/shard_map/ppermute | solution.py:11
  116.4 2.5 %collective-permute-done.16 = bf16[8,2048]{1,0:T(8,128)(2,1)S(1)} collective-permute-done((bf16[8,2048]{1,0:T(8,128)(2,1)S(1)}, bf16[8,2048]{1,0:T(8,128)(2,1)S(1)}, u32[]{:S(2)}, u32[]{:S(2)}) %collective-permute-start.16) | collective-permute-done | bytes 32800 | tf_op jit(solution)/shard_map/ppermute | solution.py:11
  118.9 1.1 collective-permute-start.15
  120.1 1.2 collective-permute-start.17
  121.3 3.6 %collective-permute-done.15 = bf16[16,2048]{1,0:T(8,128)(2,1)S(1)} collective-permute-done((bf16[16,2048]{1,0:T(8,128)(2,1)S(1)}, bf16[16,2048]{1,0:T(8,128)(2,1)S(1)}, u32[]{:S(2)}, u32[]{:S(2)}) %collective-permute-start.15) | collective-permute-done | bytes 65568 | tf_op jit(solution)/shard_map/ppermute | solution.py:11
  124.9 1.6 %collective-permute-done.17 = bf16[16,2048]{1,0:T(8,128)(2,1)S(1)} collective-permute-done((bf16[16,2048]{1,0:T(8,128)(2,1)S(1)}, bf16[16,2048]{1,0:T(8,128)(2,1)S(1)}, u32[]{:S(2)}, u32[]{:S(2)}) %collective-permute-start.17) | collective-permute-done | bytes 65568 | tf_op jit(solution)/shard_map/ppermute | solution.py:11
  126.5 0.7 add_convert_fusion.4
  (19 shorter events, 0.3 us)
Async XLA Ops:
  0.0 12.7 %collective-permute-start = (bf16[16,2048]{1,0:T(8,128)(2,1)}, bf16[16,2048]{1,0:T(8,128)(2,1)S(1)}, u32[]{:S(2)}, u32[]{:S(2)}) collective-permute-start(bf16[16,2048]{1,0:T(8,128)(2,1)} %param.4), channel_id=1, source_target_pairs={{0,2},{1,3},{2,0},{3,1},{4,6},{5,7},{6,4},{7,5},{8,10},{9,11},{10,... | collective-permute-start | bytes 196616 | tf_op jit(solution)/shard_map/ppermute | solution.py:11
  3.3 7.4 %collective-permute-start.1 = (bf16[16,2048]{1,0:T(8,128)(2,1)}, bf16[16,2048]{1,0:T(8,128)(2,1)S(1)}, u32[]{:S(2)}, u32[]{:S(2)}) collective-permute-start(bf16[16,2048]{1,0:T(8,128)(2,1)} %param.4), channel_id=1, source_target_pairs={{0,6},{1,7},{2,4},{3,5},{4,2},{5,3},{6,0},{7,1},{8,14},{9,15},{10,... | collective-permute-start | bytes 196616 | tf_op jit(solution)/shard_map/ppermute | solution.py:11
  10.7 5.2 %collective-permute-start.2 = (bf16[8,2048]{1,0:T(8,128)(2,1)S(1)}, bf16[8,2048]{1,0:T(8,128)(2,1)S(1)}, u32[]{:S(2)}, u32[]{:S(2)}) collective-permute-start(bf16[8,2048]{1,0:T(8,128)(2,1)S(1)} %slice.114), channel_id=1, source_target_pairs={{0,2},{1,3},{2,0},{3,1},{4,6},{5,7},{6,4},{7,5},{8,10},{9,11},{10,... | collective-permute-start | bytes 98312 | tf_op jit(solution)/shard_map/ppermute | solution.py:11
  12.7 6.0 %collective-permute-start.3 = (bf16[8,2048]{1,0:T(8,128)(2,1)S(1)}, bf16[8,2048]{1,0:T(8,128)(2,1)S(1)}, u32[]{:S(2)}, u32[]{:S(2)}) collective-permute-start(bf16[8,2048]{1,0:T(8,128)(2,1)S(1)} %slice.115), channel_id=1, source_target_pairs={{0,6},{1,7},{2,4},{3,5},{4,2},{5,3},{6,0},{7,1},{8,14},{9,15},{10,... | collective-permute-start | bytes 98312 | tf_op jit(solution)/shard_map/ppermute | solution.py:11
  18.8 7.7 %collective-permute-start.5 = (bf16[64,2048]{1,0:T(8,128)(2,1)S(1)}, bf16[64,2048]{1,0:T(8,128)(2,1)S(1)}, u32[]{:S(2)}, u32[]{:S(2)}) collective-permute-start(bf16[64,2048]{1,0:T(8,128)(2,1)S(1)} %get-tuple-element.29), channel_id=1, source_target_pairs={{0,24},{1,25},{2,26},{3,27},{4,28},{5,29},{6,30},{7,31},{8,16},{9,... | collective-permute-start | bytes 786440 | tf_op jit(solution)/shard_map/ppermute | solution.py:11
  21.9 7.5 %collective-permute-start.4 = (bf16[64,2048]{1,0:T(8,128)(2,1)S(1)}, bf16[64,2048]{1,0:T(8,128)(2,1)S(1)}, u32[]{:S(2)}, u32[]{:S(2)}) collective-permute-start(bf16[64,2048]{1,0:T(8,128)(2,1)S(1)} %get-tuple-element.29), channel_id=1, source_target_pairs={{0,8},{1,9},{2,10},{3,11},{4,12},{5,13},{6,14},{7,15},{8,0},{9,1},... | collective-permute-start | bytes 786440 | tf_op jit(solution)/shard_map/ppermute | solution.py:11
  26.4 5.1 %collective-permute-start.6 = (bf16[32,2048]{1,0:T(8,128)(2,1)S(1)}, bf16[32,2048]{1,0:T(8,128)(2,1)S(1)}, u32[]{:S(2)}, u32[]{:S(2)}) collective-permute-start(bf16[32,2048]{1,0:T(8,128)(2,1)S(1)} %slice.116), channel_id=1, source_target_pairs={{0,8},{1,9},{2,10},{3,11},{4,12},{5,13},{6,14},{7,15},{8,0},{9,1},... | collective-permute-start | bytes 393224 | tf_op jit(solution)/shard_map/ppermute | solution.py:11
  29.4 6.3 %collective-permute-start.7 = (bf16[32,2048]{1,0:T(8,128)(2,1)S(1)}, bf16[32,2048]{1,0:T(8,128)(2,1)S(1)}, u32[]{:S(2)}, u32[]{:S(2)}) collective-permute-start(bf16[32,2048]{1,0:T(8,128)(2,1)S(1)} %slice.117), channel_id=1, source_target_pairs={{0,24},{1,25},{2,26},{3,27},{4,28},{5,29},{6,30},{7,31},{8,16},{9,... | collective-permute-start | bytes 393224 | tf_op jit(solution)/shard_map/ppermute | solution.py:11
  29.7 8.9 %copy-start.1 = (bf16[2048,896]{1,0:T(8,128)(2,1)S(1)}, bf16[2048,896]{1,0:T(8,128)(2,1)}, u32[]{:S(2)}) copy-start(bf16[2048,896]{1,0:T(8,128)(2,1)} %param.6) | copy-start | bytes 11010052
  35.7 2.7 %collective-permute-start.8 = (bf16[256,2048]{1,0:T(8,128)(2,1)S(1)}, bf16[256,2048]{1,0:T(8,128)(2,1)S(1)}, u32[]{:S(2)}, u32[]{:S(2)}) collective-permute-start(bf16[256,2048]{1,0:T(8,128)(2,1)S(1)} %get-tuple-element.19), channel_id=1, source_target_pairs={{0,1},{1,0},{2,3},{3,2},{4,5},{5,4},{6,7},{7,6},{8,9},{9,8},{10,11... | collective-permute-start | bytes 3145736 | tf_op jit(solution)/shard_map/ppermute | solution.py:11
  72.6 17.1 %copy-start = (bf16[896,2048]{1,0:T(8,128)(2,1)S(1)}, bf16[896,2048]{1,0:T(8,128)(2,1)}, u32[]{:S(2)}) copy-start(bf16[896,2048]{1,0:T(8,128)(2,1)} %param.7) | copy-start | bytes 11010052
  91.0 2.7 %collective-permute-start.9 = (bf16[256,2048]{1,0:T(8,128)(2,1)S(1)}, bf16[256,2048]{1,0:T(8,128)(2,1)S(1)}, u32[]{:S(2)}, u32[]{:S(2)}) collective-permute-start(bf16[256,2048]{1,0:T(8,128)(2,1)S(1)} %convolution_convert_fusion), channel_id=1, source_target_pairs={{0,1},{1,0},{2,3},{3,2},{4,5},{5,4},{6,7},{7,6},{8,9},{9,8},{10,11... | collective-permute-start | bytes 3145736 | tf_op jit(solution)/shard_map/ppermute | solution.py:11
  94.1 7.0 %collective-permute-start.10 = (bf16[32,2048]{1,0:T(8,128)(2,1)S(1)}, bf16[32,2048]{1,0:T(8,128)(2,1)S(1)}, u32[]{:S(2)}, u32[]{:S(2)}) collective-permute-start(bf16[32,2048]{1,0:T(8,128)(2,1)S(1)} %get-tuple-element.8), channel_id=1, source_target_pairs={{0,24},{1,25},{2,26},{3,27},{4,28},{5,29},{6,30},{7,31},{8,16},{9,... | collective-permute-start | bytes 393224 | tf_op jit(solution)/shard_map/ppermute | solution.py:11
  94.4 6.7 %collective-permute-start.12 = (bf16[32,2048]{1,0:T(8,128)(2,1)S(1)}, bf16[32,2048]{1,0:T(8,128)(2,1)S(1)}, u32[]{:S(2)}, u32[]{:S(2)}) collective-permute-start(bf16[32,2048]{1,0:T(8,128)(2,1)S(1)} %get-tuple-element.7), channel_id=1, source_target_pairs={{0,8},{1,9},{2,10},{3,11},{4,12},{5,13},{6,14},{7,15},{8,0},{9,1},... | collective-permute-start | bytes 393224 | tf_op jit(solution)/shard_map/ppermute | solution.py:11
  101.2 7.6 %collective-permute-start.11 = (bf16[64,2048]{1,0:T(8,128)(2,1)S(1)}, bf16[64,2048]{1,0:T(8,128)(2,1)S(1)}, u32[]{:S(2)}, u32[]{:S(2)}) collective-permute-start(bf16[64,2048]{1,0:T(8,128)(2,1)S(1)} %pad_maximum_fusion), channel_id=1, source_target_pairs={{0,8},{1,9},{2,10},{3,11},{4,12},{5,13},{6,14},{7,15},{8,0},{9,1},... | collective-permute-start | bytes 786440 | tf_op jit(solution)/shard_map/ppermute | solution.py:11
  101.4 8.8 %collective-permute-start.13 = (bf16[64,2048]{1,0:T(8,128)(2,1)S(1)}, bf16[64,2048]{1,0:T(8,128)(2,1)S(1)}, u32[]{:S(2)}, u32[]{:S(2)}) collective-permute-start(bf16[64,2048]{1,0:T(8,128)(2,1)S(1)} %pad_maximum_fusion.1), channel_id=1, source_target_pairs={{0,24},{1,25},{2,26},{3,27},{4,28},{5,29},{6,30},{7,31},{8,16},{9,... | collective-permute-start | bytes 786440 | tf_op jit(solution)/shard_map/ppermute | solution.py:11
  110.3 6.1 %collective-permute-start.14 = (bf16[8,2048]{1,0:T(8,128)(2,1)S(1)}, bf16[8,2048]{1,0:T(8,128)(2,1)S(1)}, u32[]{:S(2)}, u32[]{:S(2)}) collective-permute-start(bf16[8,2048]{1,0:T(8,128)(2,1)S(1)} %get-tuple-element.16), channel_id=1, source_target_pairs={{0,6},{1,7},{2,4},{3,5},{4,2},{5,3},{6,0},{7,1},{8,14},{9,15},{10,... | collective-permute-start | bytes 98312 | tf_op jit(solution)/shard_map/ppermute | solution.py:11
  114.1 4.8 %collective-permute-start.16 = (bf16[8,2048]{1,0:T(8,128)(2,1)S(1)}, bf16[8,2048]{1,0:T(8,128)(2,1)S(1)}, u32[]{:S(2)}, u32[]{:S(2)}) collective-permute-start(bf16[8,2048]{1,0:T(8,128)(2,1)S(1)} %get-tuple-element.15), channel_id=1, source_target_pairs={{0,2},{1,3},{2,0},{3,1},{4,6},{5,7},{6,4},{7,5},{8,10},{9,11},{10,... | collective-permute-start | bytes 98312 | tf_op jit(solution)/shard_map/ppermute | solution.py:11
  118.9 6.0 %collective-permute-start.15 = (bf16[16,2048]{1,0:T(8,128)(2,1)S(1)}, bf16[16,2048]{1,0:T(8,128)(2,1)S(1)}, u32[]{:S(2)}, u32[]{:S(2)}) collective-permute-start(bf16[16,2048]{1,0:T(8,128)(2,1)S(1)} %pad_maximum_fusion.2), channel_id=1, source_target_pairs={{0,2},{1,3},{2,0},{3,1},{4,6},{5,7},{6,4},{7,5},{8,10},{9,11},{10,... | collective-permute-start | bytes 196616 | tf_op jit(solution)/shard_map/ppermute | solution.py:11
  120.1 6.5 %collective-permute-start.17 = (bf16[16,2048]{1,0:T(8,128)(2,1)S(1)}, bf16[16,2048]{1,0:T(8,128)(2,1)S(1)}, u32[]{:S(2)}, u32[]{:S(2)}) collective-permute-start(bf16[16,2048]{1,0:T(8,128)(2,1)S(1)} %pad_maximum_fusion.3), channel_id=1, source_target_pairs={{0,6},{1,7},{2,4},{3,5},{4,2},{5,3},{6,0},{7,1},{8,14},{9,15},{10,... | collective-permute-start | bytes 196616 | tf_op jit(solution)/shard_map/ppermute | solution.py:11

commit v4 on v1

v4 whole, which is shorter than its diff:
```python
import jax
import jax.numpy as jnp
from jax import lax
from jax.sharding import PartitionSpec as P

CORES, Z_PARTS, Y_PARTS = 2, 4, 4


SIZE = CORES * Z_PARTS * Y_PARTS
Z_THEN_Y = (CORES, CORES * Z_PARTS)


def swap(value, step):
    return lax.ppermute(value, "gy", [(a, a ^ step(a % CORES)) for a in range(SIZE)])


def ring_swap(value, place, i):
    return swap(value, lambda core: Z_THEN_Y[place ^ core] * i)


def core_swap(value):
    return swap(value, lambda core: 1)


def gather_ring(value, place):
    return jnp.concatenate([value] + [ring_swap(value, place, i) for i in range(1, Y_PARTS)], 0)


def reduce_ring(value, place):
    rows = value.shape[0] // Y_PARTS
    pieces = [value[i * rows:(i + 1) * rows] for i in range(Y_PARTS)]
    total = pieces[0].astype(jnp.float32)
    for i in range(1, Y_PARTS):
        total = total + ring_swap(pieces[i], place, i).astype(jnp.float32)
    return total.astype(jnp.bfloat16)


def per_device(tokens, gate_weight, up_weight, down_weight):
    width = gate_weight.shape[1]
    groups = lax.axis_size("gx")
    both = jnp.concatenate([gate_weight, up_weight], 1)
    part = gather_ring(tokens, 0)
    part = gather_ring(part, 1)
    part = jnp.concatenate([part, core_swap(part)], 0)
    term = jnp.dot(part, both, preferred_element_type=jnp.float32).astype(jnp.bfloat16)
    rows = term.shape[0] // groups
    terms = lax.all_to_all(term.reshape(groups, rows, 2 * width), "gx", 0, 0)
    summed = terms.astype(jnp.float32).sum(0)
    hidden_part = (jax.nn.silu(summed[:, :width]) * summed[:, width:]).astype(jnp.bfloat16)
    hidden = lax.all_to_all(
        jnp.broadcast_to(hidden_part[None], (groups, rows, width)), "gx", 0, 0
    ).reshape(groups * rows, width)
    half = hidden.shape[0] // 2
    theirs = jnp.dot(hidden[half:], down_weight, preferred_element_type=jnp.float32).astype(jnp.bfloat16)
    came = core_swap(theirs)
    mine = lax.optimization_barrier(
        jnp.dot(hidden[:half], down_weight, preferred_element_type=jnp.float32))
    out = (mine + came.astype(jnp.float32)).astype(jnp.bfloat16)
    out = reduce_ring(out, 1)
    return reduce_ring(out, 0)


def solution(mesh):
    in_specs = (P("gy", "gx"), P("gx", "gy"), P("gx", "gy"), P("gy", "gx"))
    out_specs = P("gy", "gx")
    return jax.shard_map(
        per_device, mesh=mesh, in_specs=in_specs, out_specs=out_specs, check_vma=False
    )
```

time: 124 us -> 118 us (0.952)
  the two profiles are of different devices: /device:TPU:2 before, /device:TPU:1 now
where the time goes in v4:
time: 118 us
  blocking collectives  45.5 us (39%)
  waiting for transfers between devices  32.2 us (27%)
  starting transfers between devices  28.2 us (24%)
  matrix products  8.64 us (7%)
  local copies, waits for them, and re-layouts  1.44 us (1%)
  other arithmetic  1.41 us (1%)
    ppermute x14, waiting for transfers between devices, swap(): lax.ppermute(value, 'gy', [(a, a ^ step(a % CORES)) for a in range(SIZE)])  32.2 us
    all_to_all x1, blocking collectives, per_device(): terms = lax.all_to_all(term.reshape(groups, rows, 2 * width), 'gx', 0, 0)  29.5 us
    ppermute x14, starting transfers between devices, swap(): lax.ppermute(value, 'gy', [(a, a ^ step(a % CORES)) for a in range(SIZE)])  28.2 us
    all_to_all x1, blocking collectives, per_device(): lax.all_to_all(jnp.broadcast_to(hidden_part[None], (groups, rows, width))...  16 us
    dot_general x1, matrix products, per_device(): jnp.dot(part, both, preferred_element_type=jnp.float32).astype(jnp.bfloat16)  6.03 us
  transfers between devices with their start and end apart: 14, of which 12 were waited for; matrix products, arithmetic and copies ran while one was open for 2% of the time, Pallas kernels for 0%

profile of v4, /device:TPU:1, one launch (start us, length us, event | category | flops | bytes accessed | tf_op | source)
XLA Modules:
  0.0 117.6 jit_solution(18152229344865475405)
XLA Ops:
  0.0 2.1 %collective-permute-start = (bf16[16,2048]{1,0:T(8,128)(2,1)}, bf16[16,2048]{1,0:T(8,128)(2,1)S(1)}, u32[]{:S(2)}, u32[]{:S(2)}) collective-permute-start(bf16[16,2048]{1,0:T(8,128)(2,1)} %param.4), channel_id=1, source_target_pairs={{0,2},{1,9},{2,0},{3,11},{4,6},{5,13},{6,4},{7,15},{8,10},{9,1},{1... | collective-permute-start | bytes 196616 | tf_op jit(solution)/shard_map/ppermute | solution.py:14
  2.1 2.6 %collective-permute-start.1 = (bf16[16,2048]{1,0:T(8,128)(2,1)}, bf16[16,2048]{1,0:T(8,128)(2,1)S(1)}, u32[]{:S(2)}, u32[]{:S(2)}) collective-permute-start(bf16[16,2048]{1,0:T(8,128)(2,1)} %param.4), channel_id=1, source_target_pairs={{0,4},{1,17},{2,6},{3,19},{4,0},{5,21},{6,2},{7,23},{8,12},{9,25},... | collective-permute-start | bytes 196616 | tf_op jit(solution)/shard_map/ppermute | solution.py:14
  4.7 0.0 collective-permute-start.2
  4.8 0.9 constant_dynamic-update-slice_fusion.10
  5.7 0.0 collective-permute-done
  5.7 1.6 %collective-permute-done.1 = bf16[16,2048]{1,0:T(8,128)(2,1)S(1)} collective-permute-done((bf16[16,2048]{1,0:T(8,128)(2,1)}, bf16[16,2048]{1,0:T(8,128)(2,1)S(1)}, u32[]{:S(2)}, u32[]{:S(2)}) %collective-permute-start.1) | collective-permute-done | bytes 65568 | tf_op jit(solution)/shard_map/ppermute | solution.py:14
  7.3 2.0 %collective-permute-done.2 = bf16[16,2048]{1,0:T(8,128)(2,1)S(1)} collective-permute-done((bf16[16,2048]{1,0:T(8,128)(2,1)}, bf16[16,2048]{1,0:T(8,128)(2,1)S(1)}, u32[]{:S(2)}, u32[]{:S(2)}) %collective-permute-start.2) | collective-permute-done | bytes 65568 | tf_op jit(solution)/shard_map/ppermute | solution.py:14
  9.3 3.1 %collective-permute-start.3 = (bf16[64,2048]{1,0:T(8,128)(2,1)S(1)}, bf16[64,2048]{1,0:T(8,128)(2,1)S(1)}, u32[]{:S(2)}, u32[]{:S(2)}) collective-permute-start(bf16[64,2048]{1,0:T(8,128)(2,1)S(1)} %get-tuple-element.21), channel_id=1, source_target_pairs={{0,8},{1,3},{2,10},{3,1},{4,12},{5,7},{6,14},{7,5},{8,0},{9,11},{1... | collective-permute-start | bytes 786440 | tf_op jit(solution)/shard_map/ppermute | solution.py:14
  12.4 5.4 %collective-permute-start.4 = (bf16[64,2048]{1,0:T(8,128)(2,1)S(1)}, bf16[64,2048]{1,0:T(8,128)(2,1)S(1)}, u32[]{:S(2)}, u32[]{:S(2)}) collective-permute-start(bf16[64,2048]{1,0:T(8,128)(2,1)S(1)} %get-tuple-element.21), channel_id=1, source_target_pairs={{0,16},{1,5},{2,18},{3,7},{4,20},{5,1},{6,22},{7,3},{8,24},{9,13},... | collective-permute-start | bytes 786440 | tf_op jit(solution)/shard_map/ppermute | solution.py:14
  17.8 0.0 collective-permute-start.5
  17.8 2.5 %collective-permute-done.3 = bf16[64,2048]{1,0:T(8,128)(2,1)S(1)} collective-permute-done((bf16[64,2048]{1,0:T(8,128)(2,1)S(1)}, bf16[64,2048]{1,0:T(8,128)(2,1)S(1)}, u32[]{:S(2)}, u32[]{:S(2)}) %collective-permute-start.3) | collective-permute-done | bytes 262176 | tf_op jit(solution)/shard_map/ppermute | solution.py:14
  20.3 0.0 copy-start.1
  20.3 7.8 %collective-permute-done.4 = bf16[64,2048]{1,0:T(8,128)(2,1)S(1)} collective-permute-done((bf16[64,2048]{1,0:T(8,128)(2,1)S(1)}, bf16[64,2048]{1,0:T(8,128)(2,1)S(1)}, u32[]{:S(2)}, u32[]{:S(2)}) %collective-permute-start.4) | collective-permute-done | bytes 262176 | tf_op jit(solution)/shard_map/ppermute | solution.py:14
  28.1 1.4 %collective-permute-done.5 = bf16[64,2048]{1,0:T(8,128)(2,1)S(1)} collective-permute-done((bf16[64,2048]{1,0:T(8,128)(2,1)S(1)}, bf16[64,2048]{1,0:T(8,128)(2,1)S(1)}, u32[]{:S(2)}, u32[]{:S(2)}) %collective-permute-start.5) | collective-permute-done | bytes 262176 | tf_op jit(solution)/shard_map/ppermute | solution.py:14
  29.6 2.7 %collective-permute-start.6 = (bf16[256,2048]{1,0:T(8,128)(2,1)S(1)}, bf16[256,2048]{1,0:T(8,128)(2,1)S(1)}, u32[]{:S(2)}, u32[]{:S(2)}) collective-permute-start(bf16[256,2048]{1,0:T(8,128)(2,1)S(1)} %get-tuple-element.13), channel_id=1, source_target_pairs={{0,1},{1,0},{2,3},{3,2},{4,5},{5,4},{6,7},{7,6},{8,9},{9,8},{10,11... | collective-permute-start | bytes 3145736 | tf_op jit(solution)/shard_map/ppermute | solution.py:14
  32.3 2.3 %collective-permute-done.6 = bf16[256,2048]{1,0:T(8,128)(2,1)S(1)} collective-permute-done((bf16[256,2048]{1,0:T(8,128)(2,1)S(1)}, bf16[256,2048]{1,0:T(8,128)(2,1)S(1)}, u32[]{:S(2)}, u32[]{:S(2)}) %collective-permute-start.6) | collective-permute-done | bytes 1048608 | tf_op jit(solution)/shard_map/ppermute | solution.py:14
  34.5 0.1 constant_dynamic-update-slice_fusion.11
  34.6 0.0 copy-done.1
  34.6 6.0 %fusion.4 = bf16[512,1792]{1,0:T(8,128)(2,1)S(1)} fusion(bf16[512,2048]{1,0:T(8,128)(2,1)S(1)} %constant_dynamic-update-slice_fusion.11, bf16[2048,896]{1,0:T(8,128)(2,1)S(1)} %copy-done.1, bf16[2048,896]{1,0:T(8,128)(2,1)} %param.5), kind=kOutput, calls=%fused_computation.5 | convolution fusion | flops 3773693952 | bytes 11272192 | tf_op jit(solution)/shard_map/dot_general | solution.py:45
  40.7 29.5 %all_to_all.10 = bf16[8,64,1792]{2,1,0:T(8,128)(2,1)S(1)} all-to-all(bf16[8,64,1792]{2,1,0:T(8,128)(2,1)S(1)} %bitcast.9), channel_id=1, replica_groups=mesh['gx'=8,'gy'=32] {'gx'}, dimensions={0} | all-to-all | bytes 3670016 | tf_op jit(solution)/shard_map/all_to_all | solution.py:47
  70.1 0.2 convert_reduce_fusion
  70.4 0.1 fusion.7
  70.5 0.0 copy-start
  70.5 0.1 broadcast_in_dim.2
  70.6 16.0 %all_to_all.11 = bf16[8,64,896]{2,1,0:T(8,128)(2,1)S(1)} all-to-all(bf16[8,64,896]{2,1,0:T(8,128)(2,1)S(1)} %broadcast_in_dim.2), channel_id=1, replica_groups=mesh['gx'=8,'gy'=32] {'gx'}, dimensions={0} | all-to-all | bytes 1835008 | tf_op jit(solution)/shard_map/all_to_all | solution.py:50
  86.6 0.1 fusion.10
  86.7 0.0 copy-done
  86.7 1.3 %convolution_convert_fusion = bf16[256,2048]{1,0:T(8,128)(2,1)S(1)} fusion(bf16[256,896]{1,0:T(8,128)(2,1)S(1)} %bitcast.10, bf16[896,2048]{1,0:T(8,128)(2,1)S(1)} %copy-done), kind=kOutput, calls=%fused_computation.6 | convolution fusion | flops 940048384 | bytes 5177344 | tf_op jit(solution)/shard_map/dot_general | solution.py:54
  88.0 2.6 %collective-permute-start.7 = (bf16[256,2048]{1,0:T(8,128)(2,1)S(1)}, bf16[256,2048]{1,0:T(8,128)(2,1)S(1)}, u32[]{:S(2)}, u32[]{:S(2)}) collective-permute-start(bf16[256,2048]{1,0:T(8,128)(2,1)S(1)} %convolution_convert_fusion), channel_id=1, source_target_pairs={{0,1},{1,0},{2,3},{3,2},{4,5},{5,4},{6,7},{7,6},{8,9},{9,8},{10,11... | collective-permute-start | bytes 3145736 | tf_op jit(solution)/shard_map/ppermute | solution.py:14
  90.6 1.3 %fusion.12 = f32[256,2048]{1,0:T(8,128)S(1)} fusion(bf16[256,896]{1,0:T(8,128)(2,1)S(1)} %bitcast.8, bf16[896,2048]{1,0:T(8,128)(2,1)S(1)} %copy-done), kind=kOutput, calls=%fused_computation.35 | convolution fusion | flops 939524096 | bytes 6225920 | tf_op jit(solution)/shard_map/dot_general | solution.py:57
  91.9 1.0 collective-permute-done.7
  92.9 0.3 add_convert_fusion
  93.2 0.1 fusion.9
  93.3 0.1 collective-permute-start.10
  93.4 1.3 %collective-permute-start.8 = (bf16[64,2048]{1,0:T(8,128)(2,1)S(1)}, bf16[64,2048]{1,0:T(8,128)(2,1)S(1)}, u32[]{:S(2)}, u32[]{:S(2)}) collective-permute-start(bf16[64,2048]{1,0:T(8,128)(2,1)S(1)} %get-tuple-element.5), channel_id=1, source_target_pairs={{0,8},{1,3},{2,10},{3,1},{4,12},{5,7},{6,14},{7,5},{8,0},{9,11},{1... | collective-permute-start | bytes 786440 | tf_op jit(solution)/shard_map/ppermute | solution.py:14
  94.7 4.4 %collective-permute-start.9 = (bf16[64,2048]{1,0:T(8,128)(2,1)S(1)}, bf16[64,2048]{1,0:T(8,128)(2,1)S(1)}, u32[]{:S(2)}, u32[]{:S(2)}) collective-permute-start(bf16[64,2048]{1,0:T(8,128)(2,1)S(1)} %get-tuple-element.7), channel_id=1, source_target_pairs={{0,16},{1,5},{2,18},{3,7},{4,20},{5,1},{6,22},{7,3},{8,24},{9,13},... | collective-permute-start | bytes 786440 | tf_op jit(solution)/shard_map/ppermute | solution.py:14
  99.0 3.6 %collective-permute-done.10 = bf16[64,2048]{1,0:T(8,128)(2,1)S(1)} collective-permute-done((bf16[64,2048]{1,0:T(8,128)(2,1)S(1)}, bf16[64,2048]{1,0:T(8,128)(2,1)S(1)}, u32[]{:S(2)}, u32[]{:S(2)}) %collective-permute-start.10) | collective-permute-done | bytes 262176 | tf_op jit(solution)/shard_map/ppermute | solution.py:14
  102.6 2.2 %collective-permute-done.8 = bf16[64,2048]{1,0:T(8,128)(2,1)S(1)} collective-permute-done((bf16[64,2048]{1,0:T(8,128)(2,1)S(1)}, bf16[64,2048]{1,0:T(8,128)(2,1)S(1)}, u32[]{:S(2)}, u32[]{:S(2)}) %collective-permute-start.8) | collective-permute-done | bytes 262176 | tf_op jit(solution)/shard_map/ppermute | solution.py:14
  104.9 6.3 %collective-permute-done.9 = bf16[64,2048]{1,0:T(8,128)(2,1)S(1)} collective-permute-done((bf16[64,2048]{1,0:T(8,128)(2,1)S(1)}, bf16[64,2048]{1,0:T(8,128)(2,1)S(1)}, u32[]{:S(2)}, u32[]{:S(2)}) %collective-permute-start.9) | collective-permute-done | bytes 262176 | tf_op jit(solution)/shard_map/ppermute | solution.py:14
  111.1 0.1 add_convert_fusion.1
  111.3 0.1 collective-permute-start.11
  111.4 0.8 collective-permute-start.12
  112.2 3.0 %collective-permute-start.13 = (bf16[16,2048]{1,0:T(8,128)(2,1)S(1)}, bf16[16,2048]{1,0:T(8,128)(2,1)S(1)}, u32[]{:S(2)}, u32[]{:S(2)}) collective-permute-start(bf16[16,2048]{1,0:T(8,128)(2,1)S(1)} %get-tuple-element.11), channel_id=1, source_target_pairs={{0,6},{1,25},{2,4},{3,27},{4,2},{5,29},{6,0},{7,31},{8,14},{9,17},... | collective-permute-start | bytes 196616 | tf_op jit(solution)/shard_map/ppermute | solution.py:14
  115.2 0.0 collective-permute-done.11
  115.2 0.9 collective-permute-done.12
  116.1 0.8 collective-permute-done.13
  116.9 0.7 add_convert_fusion.2
  (7 shorter events, 0.2 us)
Async XLA Ops:
  0.0 5.7 %collective-permute-start = (bf16[16,2048]{1,0:T(8,128)(2,1)}, bf16[16,2048]{1,0:T(8,128)(2,1)S(1)}, u32[]{:S(2)}, u32[]{:S(2)}) collective-permute-start(bf16[16,2048]{1,0:T(8,128)(2,1)} %param.4), channel_id=1, source_target_pairs={{0,2},{1,9},{2,0},{3,11},{4,6},{5,13},{6,4},{7,15},{8,10},{9,1},{1... | collective-permute-start | bytes 196616 | tf_op jit(solution)/shard_map/ppermute | solution.py:14
  2.1 5.2 %collective-permute-start.1 = (bf16[16,2048]{1,0:T(8,128)(2,1)}, bf16[16,2048]{1,0:T(8,128)(2,1)S(1)}, u32[]{:S(2)}, u32[]{:S(2)}) collective-permute-start(bf16[16,2048]{1,0:T(8,128)(2,1)} %param.4), channel_id=1, source_target_pairs={{0,4},{1,17},{2,6},{3,19},{4,0},{5,21},{6,2},{7,23},{8,12},{9,25},... | collective-permute-start | bytes 196616 | tf_op jit(solution)/shard_map/ppermute | solution.py:14
  4.7 4.5 %collective-permute-start.2 = (bf16[16,2048]{1,0:T(8,128)(2,1)}, bf16[16,2048]{1,0:T(8,128)(2,1)S(1)}, u32[]{:S(2)}, u32[]{:S(2)}) collective-permute-start(bf16[16,2048]{1,0:T(8,128)(2,1)} %param.4), channel_id=1, source_target_pairs={{0,6},{1,25},{2,4},{3,27},{4,2},{5,29},{6,0},{7,31},{8,14},{9,17},... | collective-permute-start | bytes 196616 | tf_op jit(solution)/shard_map/ppermute | solution.py:14
  9.3 11.0 %collective-permute-start.3 = (bf16[64,2048]{1,0:T(8,128)(2,1)S(1)}, bf16[64,2048]{1,0:T(8,128)(2,1)S(1)}, u32[]{:S(2)}, u32[]{:S(2)}) collective-permute-start(bf16[64,2048]{1,0:T(8,128)(2,1)S(1)} %get-tuple-element.21), channel_id=1, source_target_pairs={{0,8},{1,3},{2,10},{3,1},{4,12},{5,7},{6,14},{7,5},{8,0},{9,11},{1... | collective-permute-start | bytes 786440 | tf_op jit(solution)/shard_map/ppermute | solution.py:14
  12.4 15.7 %collective-permute-start.4 = (bf16[64,2048]{1,0:T(8,128)(2,1)S(1)}, bf16[64,2048]{1,0:T(8,128)(2,1)S(1)}, u32[]{:S(2)}, u32[]{:S(2)}) collective-permute-start(bf16[64,2048]{1,0:T(8,128)(2,1)S(1)} %get-tuple-element.21), channel_id=1, source_target_pairs={{0,16},{1,5},{2,18},{3,7},{4,20},{5,1},{6,22},{7,3},{8,24},{9,13},... | collective-permute-start | bytes 786440 | tf_op jit(solution)/shard_map/ppermute | solution.py:14
  17.8 11.7 %collective-permute-start.5 = (bf16[64,2048]{1,0:T(8,128)(2,1)S(1)}, bf16[64,2048]{1,0:T(8,128)(2,1)S(1)}, u32[]{:S(2)}, u32[]{:S(2)}) collective-permute-start(bf16[64,2048]{1,0:T(8,128)(2,1)S(1)} %get-tuple-element.21), channel_id=1, source_target_pairs={{0,24},{1,7},{2,26},{3,5},{4,28},{5,3},{6,30},{7,1},{8,16},{9,15},... | collective-permute-start | bytes 786440 | tf_op jit(solution)/shard_map/ppermute | solution.py:14
  20.3 14.4 %copy-start.1 = (bf16[2048,896]{1,0:T(8,128)(2,1)S(1)}, bf16[2048,896]{1,0:T(8,128)(2,1)}, u32[]{:S(2)}) copy-start(bf16[2048,896]{1,0:T(8,128)(2,1)} %param.6) | copy-start | bytes 11010052
  29.6 5.0 %collective-permute-start.6 = (bf16[256,2048]{1,0:T(8,128)(2,1)S(1)}, bf16[256,2048]{1,0:T(8,128)(2,1)S(1)}, u32[]{:S(2)}, u32[]{:S(2)}) collective-permute-start(bf16[256,2048]{1,0:T(8,128)(2,1)S(1)} %get-tuple-element.13), channel_id=1, source_target_pairs={{0,1},{1,0},{2,3},{3,2},{4,5},{5,4},{6,7},{7,6},{8,9},{9,8},{10,11... | collective-permute-start | bytes 3145736 | tf_op jit(solution)/shard_map/ppermute | solution.py:14
  70.5 16.2 %copy-start = (bf16[896,2048]{1,0:T(8,128)(2,1)S(1)}, bf16[896,2048]{1,0:T(8,128)(2,1)}, u32[]{:S(2)}) copy-start(bf16[896,2048]{1,0:T(8,128)(2,1)} %param.7) | copy-start | bytes 11010052
  88.0 4.9 %collective-permute-start.7 = (bf16[256,2048]{1,0:T(8,128)(2,1)S(1)}, bf16[256,2048]{1,0:T(8,128)(2,1)S(1)}, u32[]{:S(2)}, u32[]{:S(2)}) collective-permute-start(bf16[256,2048]{1,0:T(8,128)(2,1)S(1)} %convolution_convert_fusion), channel_id=1, source_target_pairs={{0,1},{1,0},{2,3},{3,2},{4,5},{5,4},{6,7},{7,6},{8,9},{9,8},{10,11... | collective-permute-start | bytes 3145736 | tf_op jit(solution)/shard_map/ppermute | solution.py:14
  93.3 9.4 %collective-permute-start.10 = (bf16[64,2048]{1,0:T(8,128)(2,1)S(1)}, bf16[64,2048]{1,0:T(8,128)(2,1)S(1)}, u32[]{:S(2)}, u32[]{:S(2)}) collective-permute-start(bf16[64,2048]{1,0:T(8,128)(2,1)S(1)} %get-tuple-element.6), channel_id=1, source_target_pairs={{0,24},{1,7},{2,26},{3,5},{4,28},{5,3},{6,30},{7,1},{8,16},{9,15},... | collective-permute-start | bytes 786440 | tf_op jit(solution)/shard_map/ppermute | solution.py:14
  93.4 11.5 %collective-permute-start.8 = (bf16[64,2048]{1,0:T(8,128)(2,1)S(1)}, bf16[64,2048]{1,0:T(8,128)(2,1)S(1)}, u32[]{:S(2)}, u32[]{:S(2)}) collective-permute-start(bf16[64,2048]{1,0:T(8,128)(2,1)S(1)} %get-tuple-element.5), channel_id=1, source_target_pairs={{0,8},{1,3},{2,10},{3,1},{4,12},{5,7},{6,14},{7,5},{8,0},{9,11},{1... | collective-permute-start | bytes 786440 | tf_op jit(solution)/shard_map/ppermute | solution.py:14
  94.7 16.5 %collective-permute-start.9 = (bf16[64,2048]{1,0:T(8,128)(2,1)S(1)}, bf16[64,2048]{1,0:T(8,128)(2,1)S(1)}, u32[]{:S(2)}, u32[]{:S(2)}) collective-permute-start(bf16[64,2048]{1,0:T(8,128)(2,1)S(1)} %get-tuple-element.7), channel_id=1, source_target_pairs={{0,16},{1,5},{2,18},{3,7},{4,20},{5,1},{6,22},{7,3},{8,24},{9,13},... | collective-permute-start | bytes 786440 | tf_op jit(solution)/shard_map/ppermute | solution.py:14
  111.3 4.0 %collective-permute-start.11 = (bf16[16,2048]{1,0:T(8,128)(2,1)S(1)}, bf16[16,2048]{1,0:T(8,128)(2,1)S(1)}, u32[]{:S(2)}, u32[]{:S(2)}) collective-permute-start(bf16[16,2048]{1,0:T(8,128)(2,1)S(1)} %get-tuple-element.10), channel_id=1, source_target_pairs={{0,2},{1,9},{2,0},{3,11},{4,6},{5,13},{6,4},{7,15},{8,10},{9,1},{1... | collective-permute-start | bytes 196616 | tf_op jit(solution)/shard_map/ppermute | solution.py:14
  111.4 4.7 %collective-permute-start.12 = (bf16[16,2048]{1,0:T(8,128)(2,1)S(1)}, bf16[16,2048]{1,0:T(8,128)(2,1)S(1)}, u32[]{:S(2)}, u32[]{:S(2)}) collective-permute-start(bf16[16,2048]{1,0:T(8,128)(2,1)S(1)} %get-tuple-element.12), channel_id=1, source_target_pairs={{0,4},{1,17},{2,6},{3,19},{4,0},{5,21},{6,2},{7,23},{8,12},{9,25},... | collective-permute-start | bytes 196616 | tf_op jit(solution)/shard_map/ppermute | solution.py:14
  112.2 4.7 %collective-permute-start.13 = (bf16[16,2048]{1,0:T(8,128)(2,1)S(1)}, bf16[16,2048]{1,0:T(8,128)(2,1)S(1)}, u32[]{:S(2)}, u32[]{:S(2)}) collective-permute-start(bf16[16,2048]{1,0:T(8,128)(2,1)S(1)} %get-tuple-element.11), channel_id=1, source_target_pairs={{0,6},{1,25},{2,4},{3,27},{4,2},{5,29},{6,0},{7,31},{8,14},{9,17},... | collective-permute-start | bytes 196616 | tf_op jit(solution)/shard_map/ppermute | solution.py:14

commit v5 on v4

v5 whole, which is shorter than its diff:
```python
import jax
import jax.numpy as jnp
from jax import lax
from jax.sharding import PartitionSpec as P

CORES, Z_PARTS, Y_PARTS = 2, 4, 4


SIZE = CORES * Z_PARTS * Y_PARTS
Z_STEP, Y_STEP = CORES, CORES * Z_PARTS
PAIRS = tuple((a * unit, (4 - a) * unit) for unit in (Z_STEP, Y_STEP) for a in (1, 3))


def swap(value, steps):
    return lax.ppermute(value, "gy", [(a, a ^ steps[a % CORES]) for a in range(SIZE)])


def core_swap(value):
    return swap(value, (1, 1))


def gather_pairs(value):
    for steps in PAIRS:
        value = jnp.concatenate([value, swap(value, steps)], 0)
    return value


def reduce_pairs(value):
    for steps in PAIRS[::-1]:
        half = value.shape[0] // 2
        came = swap(value[half:], steps)
        value = (value[:half].astype(jnp.float32) + came.astype(jnp.float32)).astype(jnp.bfloat16)
    return value


def per_device(tokens, gate_weight, up_weight, down_weight):
    width = gate_weight.shape[1]
    groups = lax.axis_size("gx")
    both = jnp.concatenate([gate_weight, up_weight], 1)
    part = gather_pairs(tokens)
    part = jnp.concatenate([part, core_swap(part)], 0)
    term = jnp.dot(part, both, preferred_element_type=jnp.float32).astype(jnp.bfloat16)
    rows = term.shape[0] // groups
    terms = lax.all_to_all(term.reshape(groups, rows, 2 * width), "gx", 0, 0)
    summed = terms.astype(jnp.float32).sum(0)
    hidden_part = (jax.nn.silu(summed[:, :width]) * summed[:, width:]).astype(jnp.bfloat16)
    hidden = lax.all_to_all(
        jnp.broadcast_to(hidden_part[None], (groups, rows, width)), "gx", 0, 0
    ).reshape(groups * rows, width)
    half = hidden.shape[0] // 2
    theirs = jnp.dot(hidden[half:], down_weight, preferred_element_type=jnp.float32).astype(jnp.bfloat16)
    came = core_swap(theirs)
    mine = lax.optimization_barrier(
        jnp.dot(hidden[:half], down_weight, preferred_element_type=jnp.float32))
    out = (mine + came.astype(jnp.float32)).astype(jnp.bfloat16)
    return reduce_pairs(out)


def solution(mesh):
    in_specs = (P("gy", "gx"), P("gx", "gy"), P("gx", "gy"), P("gy", "gx"))
    out_specs = P("gy", "gx")
    return jax.shard_map(
        per_device, mesh=mesh, in_specs=in_specs, out_specs=out_specs, check_vma=False
    )
```

time: 118 us -> 128 us (1.085)
  the two profiles are of different devices: /device:TPU:1 before, /device:TPU:2 now
where the time goes in v5:
time: 128 us; the launch traced here: 126 us
  blocking collectives  44.1 us (34%)
  waiting for transfers between devices  41.8 us (33%)
  starting transfers between devices  25.9 us (20%)
  matrix products  8.64 us (7%)
  other arithmetic  4.06 us (3%)
  local copies, waits for them, and re-layouts  1.35 us (1%)
    ppermute x10, waiting for transfers between devices, swap(): lax.ppermute(value, 'gy', [(a, a ^ steps[a % CORES]) for a in range(SIZE)])  41.8 us
    all_to_all x1, blocking collectives, per_device(): terms = lax.all_to_all(term.reshape(groups, rows, 2 * width), 'gx', 0, 0)  27.3 us
    ppermute x10, starting transfers between devices, swap(): lax.ppermute(value, 'gy', [(a, a ^ steps[a % CORES]) for a in range(SIZE)])  25.9 us
    all_to_all x1, blocking collectives, per_device(): lax.all_to_all(jnp.broadcast_to(hidden_part[None], (groups, rows, width))...  16.8 us
    dot_general x1, matrix products, per_device(): jnp.dot(part, both, preferred_element_type=jnp.float32).astype(jnp.bfloat16)  6.03 us
    concatenate x3, other arithmetic, gather_pairs(): value = jnp.concatenate([value, swap(value, steps)], 0)  2.58 us
  transfers between devices with their start and end apart: 10, of which 10 were waited for; matrix products, arithmetic and copies ran while one was open for 2% of the time, Pallas kernels for 0%

profile of v5, /device:TPU:2, one launch (start us, length us, event | category | flops | bytes accessed | tf_op | source)
XLA Modules:
  0.0 126.1 jit_solution(14255780843258148845)
XLA Ops:
  0.0 3.3 %collective-permute-start = (bf16[16,2048]{1,0:T(8,128)(2,1)}, bf16[16,2048]{1,0:T(8,128)(2,1)S(1)}, u32[]{:S(2)}, u32[]{:S(2)}) collective-permute-start(bf16[16,2048]{1,0:T(8,128)(2,1)} %param.4), channel_id=1, source_target_pairs={{0,2},{1,7},{2,0},{3,5},{4,6},{5,3},{6,4},{7,1},{8,10},{9,15},{10,... | collective-permute-start | bytes 196616 | tf_op jit(solution)/shard_map/ppermute | solution.py:15
  3.3 2.5 %collective-permute-done = bf16[16,2048]{1,0:T(8,128)(2,1)S(1)} collective-permute-done((bf16[16,2048]{1,0:T(8,128)(2,1)}, bf16[16,2048]{1,0:T(8,128)(2,1)S(1)}, u32[]{:S(2)}, u32[]{:S(2)}) %collective-permute-start) | collective-permute-done | bytes 65568 | tf_op jit(solution)/shard_map/ppermute | solution.py:15
  5.7 0.8 pad_maximum_fusion.2
  6.6 6.7 %collective-permute-start.1 = (bf16[32,2048]{1,0:T(8,128)(2,1)S(1)}, bf16[32,2048]{1,0:T(8,128)(2,1)S(1)}, u32[]{:S(2)}, u32[]{:S(2)}) collective-permute-start(bf16[32,2048]{1,0:T(8,128)(2,1)S(1)} %pad_maximum_fusion.2), channel_id=1, source_target_pairs={{0,6},{1,3},{2,4},{3,1},{4,2},{5,7},{6,0},{7,5},{8,14},{9,11},{10,... | collective-permute-start | bytes 393224 | tf_op jit(solution)/shard_map/ppermute | solution.py:15
  13.3 4.0 %collective-permute-done.1 = bf16[32,2048]{1,0:T(8,128)(2,1)S(1)} collective-permute-done((bf16[32,2048]{1,0:T(8,128)(2,1)S(1)}, bf16[32,2048]{1,0:T(8,128)(2,1)S(1)}, u32[]{:S(2)}, u32[]{:S(2)}) %collective-permute-start.1) | collective-permute-done | bytes 131104 | tf_op jit(solution)/shard_map/ppermute | solution.py:15
  17.4 0.9 pad_maximum_fusion.1
  18.2 1.7 %collective-permute-start.2 = (bf16[64,2048]{1,0:T(8,128)(2,1)S(1)}, bf16[64,2048]{1,0:T(8,128)(2,1)S(1)}, u32[]{:S(2)}, u32[]{:S(2)}) collective-permute-start(bf16[64,2048]{1,0:T(8,128)(2,1)S(1)} %pad_maximum_fusion.1), channel_id=1, source_target_pairs={{0,8},{1,25},{2,10},{3,27},{4,12},{5,29},{6,14},{7,31},{8,0},{9,17... | collective-permute-start | bytes 786440 | tf_op jit(solution)/shard_map/ppermute | solution.py:15
  19.9 0.8 constant_dynamic-update-slice_fusion.4
  20.7 3.9 %collective-permute-done.2 = bf16[64,2048]{1,0:T(8,128)(2,1)S(1)} collective-permute-done((bf16[64,2048]{1,0:T(8,128)(2,1)S(1)}, bf16[64,2048]{1,0:T(8,128)(2,1)S(1)}, u32[]{:S(2)}, u32[]{:S(2)}) %collective-permute-start.2) | collective-permute-done | bytes 262176 | tf_op jit(solution)/shard_map/ppermute | solution.py:15
  24.7 0.9 pad_maximum_fusion
  25.6 3.1 %collective-permute-start.3 = (bf16[128,2048]{1,0:T(8,128)(2,1)S(1)}, bf16[128,2048]{1,0:T(8,128)(2,1)S(1)}, u32[]{:S(2)}, u32[]{:S(2)}) collective-permute-start(bf16[128,2048]{1,0:T(8,128)(2,1)S(1)} %pad_maximum_fusion), channel_id=1, source_target_pairs={{0,24},{1,9},{2,26},{3,11},{4,28},{5,13},{6,30},{7,15},{8,16},{9,1... | collective-permute-start | bytes 1572872 | tf_op jit(solution)/shard_map/ppermute | solution.py:15
  28.7 0.0 copy-start.1
  28.8 7.3 %collective-permute-done.3 = bf16[128,2048]{1,0:T(8,128)(2,1)S(1)} collective-permute-done((bf16[128,2048]{1,0:T(8,128)(2,1)S(1)}, bf16[128,2048]{1,0:T(8,128)(2,1)S(1)}, u32[]{:S(2)}, u32[]{:S(2)}) %collective-permute-start.3) | collective-permute-done | bytes 524320 | tf_op jit(solution)/shard_map/ppermute | solution.py:15
  36.1 0.1 constant_dynamic-update-slice_fusion
  36.1 0.1 collective-permute-start.4
  36.2 2.6 %collective-permute-done.4 = bf16[256,2048]{1,0:T(8,128)(2,1)S(1)} collective-permute-done((bf16[256,2048]{1,0:T(8,128)(2,1)S(1)}, bf16[256,2048]{1,0:T(8,128)(2,1)S(1)}, u32[]{:S(2)}, u32[]{:S(2)}) %collective-permute-start.4) | collective-permute-done | bytes 1048608 | tf_op jit(solution)/shard_map/ppermute | solution.py:15
  38.9 0.1 constant_dynamic-update-slice_fusion.5
  39.0 0.0 copy-done.1
  39.0 6.0 %fusion.4 = bf16[512,1792]{1,0:T(8,128)(2,1)S(1)} fusion(bf16[512,2048]{1,0:T(8,128)(2,1)S(1)} %constant_dynamic-update-slice_fusion.5, bf16[2048,896]{1,0:T(8,128)(2,1)S(1)} %copy-done.1, bf16[2048,896]{1,0:T(8,128)(2,1)} %param.5), kind=kOutput, calls=%fused_computation.5 | convolution fusion | flops 3773693952 | bytes 11272192 | tf_op jit(solution)/shard_map/dot_general | solution.py:42
  45.0 27.3 %all_to_all.10 = bf16[8,64,1792]{2,1,0:T(8,128)(2,1)S(1)} all-to-all(bf16[8,64,1792]{2,1,0:T(8,128)(2,1)S(1)} %bitcast.9), channel_id=1, replica_groups=mesh['gx'=8,'gy'=32] {'gx'}, dimensions={0} | all-to-all | bytes 3670016 | tf_op jit(solution)/shard_map/all_to_all | solution.py:44
  72.3 0.2 convert_reduce_fusion
  72.5 0.1 fusion.7
  72.6 0.0 copy-start
  72.6 0.1 broadcast_in_dim.2
  72.8 16.8 %all_to_all.11 = bf16[8,64,896]{2,1,0:T(8,128)(2,1)S(1)} all-to-all(bf16[8,64,896]{2,1,0:T(8,128)(2,1)S(1)} %broadcast_in_dim.2), channel_id=1, replica_groups=mesh['gx'=8,'gy'=32] {'gx'}, dimensions={0} | all-to-all | bytes 1835008 | tf_op jit(solution)/shard_map/all_to_all | solution.py:47
  89.6 0.1 fusion.9
  89.7 0.0 copy-done
  89.7 1.3 %convolution_convert_fusion = bf16[256,2048]{1,0:T(8,128)(2,1)S(1)} fusion(bf16[256,896]{1,0:T(8,128)(2,1)S(1)} %bitcast.10, bf16[896,2048]{1,0:T(8,128)(2,1)S(1)} %copy-done), kind=kOutput, calls=%fused_computation.6 | convolution fusion | flops 940048384 | bytes 5177344 | tf_op jit(solution)/shard_map/dot_general | solution.py:51
  91.0 0.1 collective-permute-start.5
  91.1 1.3 %fusion.10 = f32[256,2048]{1,0:T(8,128)S(1)} fusion(bf16[256,896]{1,0:T(8,128)(2,1)S(1)} %bitcast.8, bf16[896,2048]{1,0:T(8,128)(2,1)S(1)} %copy-done), kind=kOutput, calls=%fused_computation.30 | convolution fusion | flops 939524096 | bytes 6225920 | tf_op jit(solution)/shard_map/dot_general | solution.py:54
  92.4 1.3 %collective-permute-done.5 = bf16[256,2048]{1,0:T(8,128)(2,1)S(1)} collective-permute-done((bf16[256,2048]{1,0:T(8,128)(2,1)S(1)}, bf16[256,2048]{1,0:T(8,128)(2,1)S(1)}, u32[]{:S(2)}, u32[]{:S(2)}) %collective-permute-start.5) | collective-permute-done | bytes 1048608 | tf_op jit(solution)/shard_map/ppermute | solution.py:15
  93.8 0.3 add_convert_fusion
  94.1 3.1 %collective-permute-start.6 = (bf16[128,2048]{1,0:T(8,128)(2,1)S(1)}, bf16[128,2048]{1,0:T(8,128)(2,1)S(1)}, u32[]{:S(2)}, u32[]{:S(2)}) collective-permute-start(bf16[128,2048]{1,0:T(8,128)(2,1)S(1)} %slice.61), channel_id=1, source_target_pairs={{0,24},{1,9},{2,26},{3,11},{4,28},{5,13},{6,30},{7,15},{8,16},{9,1... | collective-permute-start | bytes 1572872 | tf_op jit(solution)/shard_map/ppermute | solution.py:15
  97.2 7.4 %collective-permute-done.6 = bf16[128,2048]{1,0:T(8,128)(2,1)S(1)} collective-permute-done((bf16[128,2048]{1,0:T(8,128)(2,1)S(1)}, bf16[128,2048]{1,0:T(8,128)(2,1)S(1)}, u32[]{:S(2)}, u32[]{:S(2)}) %collective-permute-start.6) | collective-permute-done | bytes 524320 | tf_op jit(solution)/shard_map/ppermute | solution.py:15
  104.6 0.1 add_convert_fusion.1
  104.7 0.1 collective-permute-start.7
  104.8 6.4 %collective-permute-done.7 = bf16[64,2048]{1,0:T(8,128)(2,1)S(1)} collective-permute-done((bf16[64,2048]{1,0:T(8,128)(2,1)S(1)}, bf16[64,2048]{1,0:T(8,128)(2,1)S(1)}, u32[]{:S(2)}, u32[]{:S(2)}) %collective-permute-start.7) | collective-permute-done | bytes 262176 | tf_op jit(solution)/shard_map/ppermute | solution.py:15
  111.2 0.1 add_convert_fusion.2
  111.3 4.9 %collective-permute-start.8 = (bf16[32,2048]{1,0:T(8,128)(2,1)S(1)}, bf16[32,2048]{1,0:T(8,128)(2,1)S(1)}, u32[]{:S(2)}, u32[]{:S(2)}) collective-permute-start(bf16[32,2048]{1,0:T(8,128)(2,1)S(1)} %slice.65), channel_id=1, source_target_pairs={{0,6},{1,3},{2,4},{3,1},{4,2},{5,7},{6,0},{7,5},{8,14},{9,11},{10,... | collective-permute-start | bytes 393224 | tf_op jit(solution)/shard_map/ppermute | solution.py:15
  116.2 3.9 %collective-permute-done.8 = bf16[32,2048]{1,0:T(8,128)(2,1)S(1)} collective-permute-done((bf16[32,2048]{1,0:T(8,128)(2,1)S(1)}, bf16[32,2048]{1,0:T(8,128)(2,1)S(1)}, u32[]{:S(2)}, u32[]{:S(2)}) %collective-permute-start.8) | collective-permute-done | bytes 131104 | tf_op jit(solution)/shard_map/ppermute | solution.py:15
  120.2 2.8 %collective-permute-start.9 = (bf16[16,2048]{1,0:T(8,128)(2,1)S(1)}, bf16[16,2048]{1,0:T(8,128)(2,1)S(1)}, u32[]{:S(2)}, u32[]{:S(2)}) collective-permute-start(bf16[16,2048]{1,0:T(8,128)(2,1)S(1)} %slice.67), channel_id=1, source_target_pairs={{0,2},{1,7},{2,0},{3,5},{4,6},{5,3},{6,4},{7,1},{8,10},{9,15},{10,... | collective-permute-start | bytes 196616 | tf_op jit(solution)/shard_map/ppermute | solution.py:15
  123.0 2.5 %collective-permute-done.9 = bf16[16,2048]{1,0:T(8,128)(2,1)S(1)} collective-permute-done((bf16[16,2048]{1,0:T(8,128)(2,1)S(1)}, bf16[16,2048]{1,0:T(8,128)(2,1)S(1)}, u32[]{:S(2)}, u32[]{:S(2)}) %collective-permute-start.9) | collective-permute-done | bytes 65568 | tf_op jit(solution)/shard_map/ppermute | solution.py:15
  125.4 0.6 add_convert_fusion.4
  (8 shorter events, 0.2 us)
Async XLA Ops:
  0.0 5.7 %collective-permute-start = (bf16[16,2048]{1,0:T(8,128)(2,1)}, bf16[16,2048]{1,0:T(8,128)(2,1)S(1)}, u32[]{:S(2)}, u32[]{:S(2)}) collective-permute-start(bf16[16,2048]{1,0:T(8,128)(2,1)} %param.4), channel_id=1, source_target_pairs={{0,2},{1,7},{2,0},{3,5},{4,6},{5,3},{6,4},{7,1},{8,10},{9,15},{10,... | collective-permute-start | bytes 196616 | tf_op jit(solution)/shard_map/ppermute | solution.py:15
  6.6 10.8 %collective-permute-start.1 = (bf16[32,2048]{1,0:T(8,128)(2,1)S(1)}, bf16[32,2048]{1,0:T(8,128)(2,1)S(1)}, u32[]{:S(2)}, u32[]{:S(2)}) collective-permute-start(bf16[32,2048]{1,0:T(8,128)(2,1)S(1)} %pad_maximum_fusion.2), channel_id=1, source_target_pairs={{0,6},{1,3},{2,4},{3,1},{4,2},{5,7},{6,0},{7,5},{8,14},{9,11},{10,... | collective-permute-start | bytes 393224 | tf_op jit(solution)/shard_map/ppermute | solution.py:15
  18.2 6.5 %collective-permute-start.2 = (bf16[64,2048]{1,0:T(8,128)(2,1)S(1)}, bf16[64,2048]{1,0:T(8,128)(2,1)S(1)}, u32[]{:S(2)}, u32[]{:S(2)}) collective-permute-start(bf16[64,2048]{1,0:T(8,128)(2,1)S(1)} %pad_maximum_fusion.1), channel_id=1, source_target_pairs={{0,8},{1,25},{2,10},{3,27},{4,12},{5,29},{6,14},{7,31},{8,0},{9,17... | collective-permute-start | bytes 786440 | tf_op jit(solution)/shard_map/ppermute | solution.py:15
  25.6 10.5 %collective-permute-start.3 = (bf16[128,2048]{1,0:T(8,128)(2,1)S(1)}, bf16[128,2048]{1,0:T(8,128)(2,1)S(1)}, u32[]{:S(2)}, u32[]{:S(2)}) collective-permute-start(bf16[128,2048]{1,0:T(8,128)(2,1)S(1)} %pad_maximum_fusion), channel_id=1, source_target_pairs={{0,24},{1,9},{2,26},{3,11},{4,28},{5,13},{6,30},{7,15},{8,16},{9,1... | collective-permute-start | bytes 1572872 | tf_op jit(solution)/shard_map/ppermute | solution.py:15
  28.7 10.3 %copy-start.1 = (bf16[2048,896]{1,0:T(8,128)(2,1)S(1)}, bf16[2048,896]{1,0:T(8,128)(2,1)}, u32[]{:S(2)}) copy-start(bf16[2048,896]{1,0:T(8,128)(2,1)} %param.6) | copy-start | bytes 11010052
  36.1 2.7 %collective-permute-start.4 = (bf16[256,2048]{1,0:T(8,128)(2,1)S(1)}, bf16[256,2048]{1,0:T(8,128)(2,1)S(1)}, u32[]{:S(2)}, u32[]{:S(2)}) collective-permute-start(bf16[256,2048]{1,0:T(8,128)(2,1)S(1)} %get-tuple-element.7), channel_id=1, source_target_pairs={{0,1},{1,0},{2,3},{3,2},{4,5},{5,4},{6,7},{7,6},{8,9},{9,8},{10,11... | collective-permute-start | bytes 3145736 | tf_op jit(solution)/shard_map/ppermute | solution.py:15
  72.6 17.1 %copy-start = (bf16[896,2048]{1,0:T(8,128)(2,1)S(1)}, bf16[896,2048]{1,0:T(8,128)(2,1)}, u32[]{:S(2)}) copy-start(bf16[896,2048]{1,0:T(8,128)(2,1)} %param.7) | copy-start | bytes 11010052
  91.0 2.7 %collective-permute-start.5 = (bf16[256,2048]{1,0:T(8,128)(2,1)S(1)}, bf16[256,2048]{1,0:T(8,128)(2,1)S(1)}, u32[]{:S(2)}, u32[]{:S(2)}) collective-permute-start(bf16[256,2048]{1,0:T(8,128)(2,1)S(1)} %convolution_convert_fusion), channel_id=1, source_target_pairs={{0,1},{1,0},{2,3},{3,2},{4,5},{5,4},{6,7},{7,6},{8,9},{9,8},{10,11... | collective-permute-start | bytes 3145736 | tf_op jit(solution)/shard_map/ppermute | solution.py:15
  94.1 10.5 %collective-permute-start.6 = (bf16[128,2048]{1,0:T(8,128)(2,1)S(1)}, bf16[128,2048]{1,0:T(8,128)(2,1)S(1)}, u32[]{:S(2)}, u32[]{:S(2)}) collective-permute-start(bf16[128,2048]{1,0:T(8,128)(2,1)S(1)} %slice.61), channel_id=1, source_target_pairs={{0,24},{1,9},{2,26},{3,11},{4,28},{5,13},{6,30},{7,15},{8,16},{9,1... | collective-permute-start | bytes 1572872 | tf_op jit(solution)/shard_map/ppermute | solution.py:15
  104.7 6.5 %collective-permute-start.7 = (bf16[64,2048]{1,0:T(8,128)(2,1)S(1)}, bf16[64,2048]{1,0:T(8,128)(2,1)S(1)}, u32[]{:S(2)}, u32[]{:S(2)}) collective-permute-start(bf16[64,2048]{1,0:T(8,128)(2,1)S(1)} %slice.63), channel_id=1, source_target_pairs={{0,8},{1,25},{2,10},{3,27},{4,12},{5,29},{6,14},{7,31},{8,0},{9,17... | collective-permute-start | bytes 786440 | tf_op jit(solution)/shard_map/ppermute | solution.py:15
  111.3 8.8 %collective-permute-start.8 = (bf16[32,2048]{1,0:T(8,128)(2,1)S(1)}, bf16[32,2048]{1,0:T(8,128)(2,1)S(1)}, u32[]{:S(2)}, u32[]{:S(2)}) collective-permute-start(bf16[32,2048]{1,0:T(8,128)(2,1)S(1)} %slice.65), channel_id=1, source_target_pairs={{0,6},{1,3},{2,4},{3,1},{4,2},{5,7},{6,0},{7,5},{8,14},{9,11},{10,... | collective-permute-start | bytes 393224 | tf_op jit(solution)/shard_map/ppermute | solution.py:15
  120.2 5.3 %collective-permute-start.9 = (bf16[16,2048]{1,0:T(8,128)(2,1)S(1)}, bf16[16,2048]{1,0:T(8,128)(2,1)S(1)}, u32[]{:S(2)}, u32[]{:S(2)}) collective-permute-start(bf16[16,2048]{1,0:T(8,128)(2,1)S(1)} %slice.67), channel_id=1, source_target_pairs={{0,2},{1,7},{2,0},{3,5},{4,6},{5,3},{6,4},{7,1},{8,10},{9,15},{10,... | collective-permute-start | bytes 196616 | tf_op jit(solution)/shard_map/ppermute | solution.py:15

commit v6 on v4

--- a/solution.py
+++ b/solution.py
@@ -8,6 +8,7 @@
 
 SIZE = CORES * Z_PARTS * Y_PARTS
 Z_THEN_Y = (CORES, CORES * Z_PARTS)
+NEAR_FIRST = (1, 3, 2)
 
 
 def swap(value, step):
@@ -23,15 +24,15 @@
 
 
 def gather_ring(value, place):
-    return jnp.concatenate([value] + [ring_swap(value, place, i) for i in range(1, Y_PARTS)], 0)
+    return jnp.concatenate([value] + [ring_swap(value, place, i) for i in NEAR_FIRST], 0)
 
 
-def reduce_ring(value, place):
+def reduce_ring(value, place, order):
     rows = value.shape[0] // Y_PARTS
     pieces = [value[i * rows:(i + 1) * rows] for i in range(Y_PARTS)]
     total = pieces[0].astype(jnp.float32)
-    for i in range(1, Y_PARTS):
-        total = total + ring_swap(pieces[i], place, i).astype(jnp.float32)
+    for i in order:
+        total = total + ring_swap(pieces[1 + NEAR_FIRST.index(i)], place, i).astype(jnp.float32)
     return total.astype(jnp.bfloat16)
 
 
@@ -56,8 +57,8 @@
     mine = lax.optimization_barrier(
         jnp.dot(hidden[:half], down_weight, preferred_element_type=jnp.float32))
     out = (mine + came.astype(jnp.float32)).astype(jnp.bfloat16)
-    out = reduce_ring(out, 1)
-    return reduce_ring(out, 0)
+    out = reduce_ring(out, 1, (1, 2, 3))
+    return reduce_ring(out, 0, NEAR_FIRST)
 
 
 def solution(mesh):

time: 118 us -> 115 us (0.975)
  blocking collectives: 45.5 us -> 44.1 us
    all_to_all x1, blocking collectives: 29.5 us -> 28.1 us  [per_device(): terms = lax.all_to_all(term.reshape(groups, rows, 2 * width), 'gx', 0, 0)]
  transfers between devices with their start and end apart: 14 -> 14, of which waited for: 12 -> 11; matrix products, arithmetic and copies ran while one was open for 2% -> 2% of each run, Pallas kernels for 0% -> 0%
where the time goes in v6:
time: 115 us
  blocking collectives  44.1 us (38%)
  waiting for transfers between devices  32.2 us (28%)
  starting transfers between devices  27.1 us (24%)
  matrix products  8.64 us (8%)
  local copies, waits for them, and re-layouts  1.41 us (1%)
  other arithmetic  1.41 us (1%)
    ppermute x14, waiting for transfers between devices, swap(): lax.ppermute(value, 'gy', [(a, a ^ step(a % CORES)) for a in range(SIZE)])  32.2 us
    all_to_all x1, blocking collectives, per_device(): terms = lax.all_to_all(term.reshape(groups, rows, 2 * width), 'gx', 0, 0)  28.1 us
    ppermute x14, starting transfers between devices, swap(): lax.ppermute(value, 'gy', [(a, a ^ step(a % CORES)) for a in range(SIZE)])  27.1 us
    all_to_all x1, blocking collectives, per_device(): lax.all_to_all(jnp.broadcast_to(hidden_part[None], (groups, rows, width))...  16 us
    dot_general x1, matrix products, per_device(): jnp.dot(part, both, preferred_element_type=jnp.float32).astype(jnp.bfloat16)  6.03 us
  transfers between devices with their start and end apart: 14, of which 11 were waited for; matrix products, arithmetic and copies ran while one was open for 2% of the time, Pallas kernels for 0%

profile of v6, /device:TPU:1, one launch (start us, length us, event | category | flops | bytes accessed | tf_op | source)
XLA Modules:
  0.0 115.0 jit_solution(14946486838550414741)
XLA Ops:
  0.0 2.1 %collective-permute-start = (bf16[16,2048]{1,0:T(8,128)(2,1)}, bf16[16,2048]{1,0:T(8,128)(2,1)S(1)}, u32[]{:S(2)}, u32[]{:S(2)}) collective-permute-start(bf16[16,2048]{1,0:T(8,128)(2,1)} %param.4), channel_id=1, source_target_pairs={{0,2},{1,9},{2,0},{3,11},{4,6},{5,13},{6,4},{7,15},{8,10},{9,1},{1... | collective-permute-start | bytes 196616 | tf_op jit(solution)/shard_map/ppermute | solution.py:15
  2.1 1.9 %collective-permute-start.1 = (bf16[16,2048]{1,0:T(8,128)(2,1)}, bf16[16,2048]{1,0:T(8,128)(2,1)S(1)}, u32[]{:S(2)}, u32[]{:S(2)}) collective-permute-start(bf16[16,2048]{1,0:T(8,128)(2,1)} %param.4), channel_id=1, source_target_pairs={{0,6},{1,25},{2,4},{3,27},{4,2},{5,29},{6,0},{7,31},{8,14},{9,17},... | collective-permute-start | bytes 196616 | tf_op jit(solution)/shard_map/ppermute | solution.py:15
  4.0 0.7 collective-permute-start.2
  4.8 0.9 constant_dynamic-update-slice_fusion.10
  5.6 0.0 collective-permute-done
  5.7 1.0 collective-permute-done.1
  6.7 2.2 %collective-permute-done.2 = bf16[16,2048]{1,0:T(8,128)(2,1)S(1)} collective-permute-done((bf16[16,2048]{1,0:T(8,128)(2,1)}, bf16[16,2048]{1,0:T(8,128)(2,1)S(1)}, u32[]{:S(2)}, u32[]{:S(2)}) %collective-permute-start.2) | collective-permute-done | bytes 65568 | tf_op jit(solution)/shard_map/ppermute | solution.py:15
  8.9 3.4 %collective-permute-start.3 = (bf16[64,2048]{1,0:T(8,128)(2,1)S(1)}, bf16[64,2048]{1,0:T(8,128)(2,1)S(1)}, u32[]{:S(2)}, u32[]{:S(2)}) collective-permute-start(bf16[64,2048]{1,0:T(8,128)(2,1)S(1)} %get-tuple-element.21), channel_id=1, source_target_pairs={{0,8},{1,3},{2,10},{3,1},{4,12},{5,7},{6,14},{7,5},{8,0},{9,11},{1... | collective-permute-start | bytes 786440 | tf_op jit(solution)/shard_map/ppermute | solution.py:15
  12.3 4.2 %collective-permute-start.4 = (bf16[64,2048]{1,0:T(8,128)(2,1)S(1)}, bf16[64,2048]{1,0:T(8,128)(2,1)S(1)}, u32[]{:S(2)}, u32[]{:S(2)}) collective-permute-start(bf16[64,2048]{1,0:T(8,128)(2,1)S(1)} %get-tuple-element.21), channel_id=1, source_target_pairs={{0,24},{1,7},{2,26},{3,5},{4,28},{5,3},{6,30},{7,1},{8,16},{9,15},... | collective-permute-start | bytes 786440 | tf_op jit(solution)/shard_map/ppermute | solution.py:15
  16.5 0.9 collective-permute-start.5
  17.4 3.0 %collective-permute-done.3 = bf16[64,2048]{1,0:T(8,128)(2,1)S(1)} collective-permute-done((bf16[64,2048]{1,0:T(8,128)(2,1)S(1)}, bf16[64,2048]{1,0:T(8,128)(2,1)S(1)}, u32[]{:S(2)}, u32[]{:S(2)}) %collective-permute-start.3) | collective-permute-done | bytes 262176 | tf_op jit(solution)/shard_map/ppermute | solution.py:15
  20.3 0.0 copy-start.1
  20.4 7.8 %collective-permute-done.4 = bf16[64,2048]{1,0:T(8,128)(2,1)S(1)} collective-permute-done((bf16[64,2048]{1,0:T(8,128)(2,1)S(1)}, bf16[64,2048]{1,0:T(8,128)(2,1)S(1)}, u32[]{:S(2)}, u32[]{:S(2)}) %collective-permute-start.4) | collective-permute-done | bytes 262176 | tf_op jit(solution)/shard_map/ppermute | solution.py:15
  28.2 0.0 collective-permute-done.5
  28.3 2.2 %collective-permute-start.6 = (bf16[256,2048]{1,0:T(8,128)(2,1)S(1)}, bf16[256,2048]{1,0:T(8,128)(2,1)S(1)}, u32[]{:S(2)}, u32[]{:S(2)}) collective-permute-start(bf16[256,2048]{1,0:T(8,128)(2,1)S(1)} %get-tuple-element.13), channel_id=1, source_target_pairs={{0,1},{1,0},{2,3},{3,2},{4,5},{5,4},{6,7},{7,6},{8,9},{9,8},{10,11... | collective-permute-start | bytes 3145736 | tf_op jit(solution)/shard_map/ppermute | solution.py:15
  30.5 2.3 %collective-permute-done.6 = bf16[256,2048]{1,0:T(8,128)(2,1)S(1)} collective-permute-done((bf16[256,2048]{1,0:T(8,128)(2,1)S(1)}, bf16[256,2048]{1,0:T(8,128)(2,1)S(1)}, u32[]{:S(2)}, u32[]{:S(2)}) %collective-permute-start.6) | collective-permute-done | bytes 1048608 | tf_op jit(solution)/shard_map/ppermute | solution.py:15
  32.8 0.1 constant_dynamic-update-slice_fusion.11
  32.9 0.0 copy-done.1
  32.9 6.0 %fusion.4 = bf16[512,1792]{1,0:T(8,128)(2,1)S(1)} fusion(bf16[512,2048]{1,0:T(8,128)(2,1)S(1)} %constant_dynamic-update-slice_fusion.11, bf16[2048,896]{1,0:T(8,128)(2,1)S(1)} %copy-done.1, bf16[2048,896]{1,0:T(8,128)(2,1)} %param.5), kind=kOutput, calls=%fused_computation.5 | convolution fusion | flops 3773693952 | bytes 11272192 | tf_op jit(solution)/shard_map/dot_general | solution.py:46
  38.9 28.1 %all_to_all.10 = bf16[8,64,1792]{2,1,0:T(8,128)(2,1)S(1)} all-to-all(bf16[8,64,1792]{2,1,0:T(8,128)(2,1)S(1)} %bitcast.9), channel_id=1, replica_groups=mesh['gx'=8,'gy'=32] {'gx'}, dimensions={0} | all-to-all | bytes 3670016 | tf_op jit(solution)/shard_map/all_to_all | solution.py:48
  67.0 0.2 convert_reduce_fusion
  67.2 0.1 fusion.7
  67.3 0.0 copy-start
  67.3 0.1 broadcast_in_dim.2
  67.4 16.0 %all_to_all.11 = bf16[8,64,896]{2,1,0:T(8,128)(2,1)S(1)} all-to-all(bf16[8,64,896]{2,1,0:T(8,128)(2,1)S(1)} %broadcast_in_dim.2), channel_id=1, replica_groups=mesh['gx'=8,'gy'=32] {'gx'}, dimensions={0} | all-to-all | bytes 1835008 | tf_op jit(solution)/shard_map/all_to_all | solution.py:51
  83.5 0.1 fusion.10
  83.6 0.0 copy-done
  83.6 1.3 %convolution_convert_fusion = bf16[256,2048]{1,0:T(8,128)(2,1)S(1)} fusion(bf16[256,896]{1,0:T(8,128)(2,1)S(1)} %bitcast.10, bf16[896,2048]{1,0:T(8,128)(2,1)S(1)} %copy-done), kind=kOutput, calls=%fused_computation.6 | convolution fusion | flops 940048384 | bytes 5177344 | tf_op jit(solution)/shard_map/dot_general | solution.py:55
  84.9 2.6 %collective-permute-start.7 = (bf16[256,2048]{1,0:T(8,128)(2,1)S(1)}, bf16[256,2048]{1,0:T(8,128)(2,1)S(1)}, u32[]{:S(2)}, u32[]{:S(2)}) collective-permute-start(bf16[256,2048]{1,0:T(8,128)(2,1)S(1)} %convolution_convert_fusion), channel_id=1, source_target_pairs={{0,1},{1,0},{2,3},{3,2},{4,5},{5,4},{6,7},{7,6},{8,9},{9,8},{10,11... | collective-permute-start | bytes 3145736 | tf_op jit(solution)/shard_map/ppermute | solution.py:15
  87.5 1.3 %fusion.12 = f32[256,2048]{1,0:T(8,128)S(1)} fusion(bf16[256,896]{1,0:T(8,128)(2,1)S(1)} %bitcast.8, bf16[896,2048]{1,0:T(8,128)(2,1)S(1)} %copy-done), kind=kOutput, calls=%fused_computation.35 | convolution fusion | flops 939524096 | bytes 6225920 | tf_op jit(solution)/shard_map/dot_general | solution.py:58
  88.8 1.0 collective-permute-done.7
  89.8 0.3 add_convert_fusion
  90.0 0.1 fusion.9
  90.1 2.2 %collective-permute-start.10 = (bf16[64,2048]{1,0:T(8,128)(2,1)S(1)}, bf16[64,2048]{1,0:T(8,128)(2,1)S(1)}, u32[]{:S(2)}, u32[]{:S(2)}) collective-permute-start(bf16[64,2048]{1,0:T(8,128)(2,1)S(1)} %get-tuple-element.6), channel_id=1, source_target_pairs={{0,24},{1,7},{2,26},{3,5},{4,28},{5,3},{6,30},{7,1},{8,16},{9,15},... | collective-permute-start | bytes 786440 | tf_op jit(solution)/shard_map/ppermute | solution.py:15
  92.3 1.1 collective-permute-start.8
  93.4 2.5 %collective-permute-start.9 = (bf16[64,2048]{1,0:T(8,128)(2,1)S(1)}, bf16[64,2048]{1,0:T(8,128)(2,1)S(1)}, u32[]{:S(2)}, u32[]{:S(2)}) collective-permute-start(bf16[64,2048]{1,0:T(8,128)(2,1)S(1)} %get-tuple-element.7), channel_id=1, source_target_pairs={{0,16},{1,5},{2,18},{3,7},{4,20},{5,1},{6,22},{7,3},{8,24},{9,13},... | collective-permute-start | bytes 786440 | tf_op jit(solution)/shard_map/ppermute | solution.py:15
  95.9 6.0 %collective-permute-done.10 = bf16[64,2048]{1,0:T(8,128)(2,1)S(1)} collective-permute-done((bf16[64,2048]{1,0:T(8,128)(2,1)S(1)}, bf16[64,2048]{1,0:T(8,128)(2,1)S(1)}, u32[]{:S(2)}, u32[]{:S(2)}) %collective-permute-start.10) | collective-permute-done | bytes 262176 | tf_op jit(solution)/shard_map/ppermute | solution.py:15
  101.9 2.5 %collective-permute-done.8 = bf16[64,2048]{1,0:T(8,128)(2,1)S(1)} collective-permute-done((bf16[64,2048]{1,0:T(8,128)(2,1)S(1)}, bf16[64,2048]{1,0:T(8,128)(2,1)S(1)}, u32[]{:S(2)}, u32[]{:S(2)}) %collective-permute-start.8) | collective-permute-done | bytes 262176 | tf_op jit(solution)/shard_map/ppermute | solution.py:15
  104.4 3.5 %collective-permute-done.9 = bf16[64,2048]{1,0:T(8,128)(2,1)S(1)} collective-permute-done((bf16[64,2048]{1,0:T(8,128)(2,1)S(1)}, bf16[64,2048]{1,0:T(8,128)(2,1)S(1)}, u32[]{:S(2)}, u32[]{:S(2)}) %collective-permute-start.9) | collective-permute-done | bytes 262176 | tf_op jit(solution)/shard_map/ppermute | solution.py:15
  107.9 0.1 add_convert_fusion.1
  108.1 0.1 collective-permute-start.11
  108.2 1.5 %collective-permute-start.12 = (bf16[16,2048]{1,0:T(8,128)(2,1)S(1)}, bf16[16,2048]{1,0:T(8,128)(2,1)S(1)}, u32[]{:S(2)}, u32[]{:S(2)}) collective-permute-start(bf16[16,2048]{1,0:T(8,128)(2,1)S(1)} %get-tuple-element.12), channel_id=1, source_target_pairs={{0,6},{1,25},{2,4},{3,27},{4,2},{5,29},{6,0},{7,31},{8,14},{9,17},... | collective-permute-start | bytes 196616 | tf_op jit(solution)/shard_map/ppermute | solution.py:15
  109.7 1.7 %collective-permute-start.13 = (bf16[16,2048]{1,0:T(8,128)(2,1)S(1)}, bf16[16,2048]{1,0:T(8,128)(2,1)S(1)}, u32[]{:S(2)}, u32[]{:S(2)}) collective-permute-start(bf16[16,2048]{1,0:T(8,128)(2,1)S(1)} %get-tuple-element.11), channel_id=1, source_target_pairs={{0,4},{1,17},{2,6},{3,19},{4,0},{5,21},{6,2},{7,23},{8,12},{9,25},... | collective-permute-start | bytes 196616 | tf_op jit(solution)/shard_map/ppermute | solution.py:15
  111.4 0.0 collective-permute-done.11
  111.4 1.5 %collective-permute-done.12 = bf16[16,2048]{1,0:T(8,128)(2,1)S(1)} collective-permute-done((bf16[16,2048]{1,0:T(8,128)(2,1)S(1)}, bf16[16,2048]{1,0:T(8,128)(2,1)S(1)}, u32[]{:S(2)}, u32[]{:S(2)}) %collective-permute-start.12) | collective-permute-done | bytes 65568 | tf_op jit(solution)/shard_map/ppermute | solution.py:15
  112.9 1.4 %collective-permute-done.13 = bf16[16,2048]{1,0:T(8,128)(2,1)S(1)} collective-permute-done((bf16[16,2048]{1,0:T(8,128)(2,1)S(1)}, bf16[16,2048]{1,0:T(8,128)(2,1)S(1)}, u32[]{:S(2)}, u32[]{:S(2)}) %collective-permute-start.13) | collective-permute-done | bytes 65568 | tf_op jit(solution)/shard_map/ppermute | solution.py:15
  114.4 0.7 add_convert_fusion.2
  (7 shorter events, 0.2 us)
Async XLA Ops:
  0.0 5.6 %collective-permute-start = (bf16[16,2048]{1,0:T(8,128)(2,1)}, bf16[16,2048]{1,0:T(8,128)(2,1)S(1)}, u32[]{:S(2)}, u32[]{:S(2)}) collective-permute-start(bf16[16,2048]{1,0:T(8,128)(2,1)} %param.4), channel_id=1, source_target_pairs={{0,2},{1,9},{2,0},{3,11},{4,6},{5,13},{6,4},{7,15},{8,10},{9,1},{1... | collective-permute-start | bytes 196616 | tf_op jit(solution)/shard_map/ppermute | solution.py:15
  2.1 4.5 %collective-permute-start.1 = (bf16[16,2048]{1,0:T(8,128)(2,1)}, bf16[16,2048]{1,0:T(8,128)(2,1)S(1)}, u32[]{:S(2)}, u32[]{:S(2)}) collective-permute-start(bf16[16,2048]{1,0:T(8,128)(2,1)} %param.4), channel_id=1, source_target_pairs={{0,6},{1,25},{2,4},{3,27},{4,2},{5,29},{6,0},{7,31},{8,14},{9,17},... | collective-permute-start | bytes 196616 | tf_op jit(solution)/shard_map/ppermute | solution.py:15
  4.0 4.8 %collective-permute-start.2 = (bf16[16,2048]{1,0:T(8,128)(2,1)}, bf16[16,2048]{1,0:T(8,128)(2,1)S(1)}, u32[]{:S(2)}, u32[]{:S(2)}) collective-permute-start(bf16[16,2048]{1,0:T(8,128)(2,1)} %param.4), channel_id=1, source_target_pairs={{0,4},{1,17},{2,6},{3,19},{4,0},{5,21},{6,2},{7,23},{8,12},{9,25},... | collective-permute-start | bytes 196616 | tf_op jit(solution)/shard_map/ppermute | solution.py:15
  8.9 11.5 %collective-permute-start.3 = (bf16[64,2048]{1,0:T(8,128)(2,1)S(1)}, bf16[64,2048]{1,0:T(8,128)(2,1)S(1)}, u32[]{:S(2)}, u32[]{:S(2)}) collective-permute-start(bf16[64,2048]{1,0:T(8,128)(2,1)S(1)} %get-tuple-element.21), channel_id=1, source_target_pairs={{0,8},{1,3},{2,10},{3,1},{4,12},{5,7},{6,14},{7,5},{8,0},{9,11},{1... | collective-permute-start | bytes 786440 | tf_op jit(solution)/shard_map/ppermute | solution.py:15
  12.3 15.9 %collective-permute-start.4 = (bf16[64,2048]{1,0:T(8,128)(2,1)S(1)}, bf16[64,2048]{1,0:T(8,128)(2,1)S(1)}, u32[]{:S(2)}, u32[]{:S(2)}) collective-permute-start(bf16[64,2048]{1,0:T(8,128)(2,1)S(1)} %get-tuple-element.21), channel_id=1, source_target_pairs={{0,24},{1,7},{2,26},{3,5},{4,28},{5,3},{6,30},{7,1},{8,16},{9,15},... | collective-permute-start | bytes 786440 | tf_op jit(solution)/shard_map/ppermute | solution.py:15
  16.5 11.8 %collective-permute-start.5 = (bf16[64,2048]{1,0:T(8,128)(2,1)S(1)}, bf16[64,2048]{1,0:T(8,128)(2,1)S(1)}, u32[]{:S(2)}, u32[]{:S(2)}) collective-permute-start(bf16[64,2048]{1,0:T(8,128)(2,1)S(1)} %get-tuple-element.21), channel_id=1, source_target_pairs={{0,16},{1,5},{2,18},{3,7},{4,20},{5,1},{6,22},{7,3},{8,24},{9,13},... | collective-permute-start | bytes 786440 | tf_op jit(solution)/shard_map/ppermute | solution.py:15
  20.3 12.5 %copy-start.1 = (bf16[2048,896]{1,0:T(8,128)(2,1)S(1)}, bf16[2048,896]{1,0:T(8,128)(2,1)}, u32[]{:S(2)}) copy-start(bf16[2048,896]{1,0:T(8,128)(2,1)} %param.6) | copy-start | bytes 11010052
  28.3 4.5 %collective-permute-start.6 = (bf16[256,2048]{1,0:T(8,128)(2,1)S(1)}, bf16[256,2048]{1,0:T(8,128)(2,1)S(1)}, u32[]{:S(2)}, u32[]{:S(2)}) collective-permute-start(bf16[256,2048]{1,0:T(8,128)(2,1)S(1)} %get-tuple-element.13), channel_id=1, source_target_pairs={{0,1},{1,0},{2,3},{3,2},{4,5},{5,4},{6,7},{7,6},{8,9},{9,8},{10,11... | collective-permute-start | bytes 3145736 | tf_op jit(solution)/shard_map/ppermute | solution.py:15
  67.3 16.3 %copy-start = (bf16[896,2048]{1,0:T(8,128)(2,1)S(1)}, bf16[896,2048]{1,0:T(8,128)(2,1)}, u32[]{:S(2)}) copy-start(bf16[896,2048]{1,0:T(8,128)(2,1)} %param.7) | copy-start | bytes 11010052
  84.9 4.9 %collective-permute-start.7 = (bf16[256,2048]{1,0:T(8,128)(2,1)S(1)}, bf16[256,2048]{1,0:T(8,128)(2,1)S(1)}, u32[]{:S(2)}, u32[]{:S(2)}) collective-permute-start(bf16[256,2048]{1,0:T(8,128)(2,1)S(1)} %convolution_convert_fusion), channel_id=1, source_target_pairs={{0,1},{1,0},{2,3},{3,2},{4,5},{5,4},{6,7},{7,6},{8,9},{9,8},{10,11... | collective-permute-start | bytes 3145736 | tf_op jit(solution)/shard_map/ppermute | solution.py:15
  90.1 11.8 %collective-permute-start.10 = (bf16[64,2048]{1,0:T(8,128)(2,1)S(1)}, bf16[64,2048]{1,0:T(8,128)(2,1)S(1)}, u32[]{:S(2)}, u32[]{:S(2)}) collective-permute-start(bf16[64,2048]{1,0:T(8,128)(2,1)S(1)} %get-tuple-element.6), channel_id=1, source_target_pairs={{0,24},{1,7},{2,26},{3,5},{4,28},{5,3},{6,30},{7,1},{8,16},{9,15},... | collective-permute-start | bytes 786440 | tf_op jit(solution)/shard_map/ppermute | solution.py:15
  92.3 12.1 %collective-permute-start.8 = (bf16[64,2048]{1,0:T(8,128)(2,1)S(1)}, bf16[64,2048]{1,0:T(8,128)(2,1)S(1)}, u32[]{:S(2)}, u32[]{:S(2)}) collective-permute-start(bf16[64,2048]{1,0:T(8,128)(2,1)S(1)} %get-tuple-element.5), channel_id=1, source_target_pairs={{0,8},{1,3},{2,10},{3,1},{4,12},{5,7},{6,14},{7,5},{8,0},{9,11},{1... | collective-permute-start | bytes 786440 | tf_op jit(solution)/shard_map/ppermute | solution.py:15
  93.4 14.5 %collective-permute-start.9 = (bf16[64,2048]{1,0:T(8,128)(2,1)S(1)}, bf16[64,2048]{1,0:T(8,128)(2,1)S(1)}, u32[]{:S(2)}, u32[]{:S(2)}) collective-permute-start(bf16[64,2048]{1,0:T(8,128)(2,1)S(1)} %get-tuple-element.7), channel_id=1, source_target_pairs={{0,16},{1,5},{2,18},{3,7},{4,20},{5,1},{6,22},{7,3},{8,24},{9,13},... | collective-permute-start | bytes 786440 | tf_op jit(solution)/shard_map/ppermute | solution.py:15
  108.1 3.3 %collective-permute-start.11 = (bf16[16,2048]{1,0:T(8,128)(2,1)S(1)}, bf16[16,2048]{1,0:T(8,128)(2,1)S(1)}, u32[]{:S(2)}, u32[]{:S(2)}) collective-permute-start(bf16[16,2048]{1,0:T(8,128)(2,1)S(1)} %get-tuple-element.10), channel_id=1, source_target_pairs={{0,2},{1,9},{2,0},{3,11},{4,6},{5,13},{6,4},{7,15},{8,10},{9,1},{1... | collective-permute-start | bytes 196616 | tf_op jit(solution)/shard_map/ppermute | solution.py:15
  108.2 4.7 %collective-permute-start.12 = (bf16[16,2048]{1,0:T(8,128)(2,1)S(1)}, bf16[16,2048]{1,0:T(8,128)(2,1)S(1)}, u32[]{:S(2)}, u32[]{:S(2)}) collective-permute-start(bf16[16,2048]{1,0:T(8,128)(2,1)S(1)} %get-tuple-element.12), channel_id=1, source_target_pairs={{0,6},{1,25},{2,4},{3,27},{4,2},{5,29},{6,0},{7,31},{8,14},{9,17},... | collective-permute-start | bytes 196616 | tf_op jit(solution)/shard_map/ppermute | solution.py:15
  109.7 4.6 %collective-permute-start.13 = (bf16[16,2048]{1,0:T(8,128)(2,1)S(1)}, bf16[16,2048]{1,0:T(8,128)(2,1)S(1)}, u32[]{:S(2)}, u32[]{:S(2)}) collective-permute-start(bf16[16,2048]{1,0:T(8,128)(2,1)S(1)} %get-tuple-element.11), channel_id=1, source_target_pairs={{0,4},{1,17},{2,6},{3,19},{4,0},{5,21},{6,2},{7,23},{8,12},{9,25},... | collective-permute-start | bytes 196616 | tf_op jit(solution)/shard_map/ppermute | solution.py:15
